TPU v7x, 128 devices: a whole 4x4x4 slice. The times are simulated.
128 devices in a mesh: gx: 16 (over z, x), gy: 8 (over y, core).
Axes of the slice: x: 4, y: 4, z: 4, core: 2. Of those that a mesh axis runs over, the one named last changes fastest.
Arguments:
- inputs: float32 [128, 64, 16, 256], P('gx', 'gy'), may hold values from -6 to 6
- cotangent: float32 [128, 64, 16, 256], P('gx', 'gy'), may hold values from -6 to 6
- weight: float32 [6912, 256], replicated, may hold values from -0.125 to 0.125
- occupancy: int32 [128, 64, 16], P('gx', 'gy'), may hold values from 0 to 1, as said below
Outputs:
- input_grad: float32 [128, 64, 16, 256], P('gx', 'gy')
- weight_grad: float32 [6912, 256], P('gx', 'gy')
Inputs may be any that keep to these rules, and one draw needn't show every extreme that they name: `occupancy`: occupied voxels lie in bricks of 8 x 8 x min(8, 16) voxels aligned to each device's block; some bricks are empty.
All inputs are finite; a program needn't handle non-finite values.
Results may differ from a plain program's by a relative error of at most 0.0001.
Values sent between devices are 32-bit elements; how exact they have to be, the bound alone decides.
A program may use at most 192 MiB of HBM per device.

v0:
```python
import jax
import jax.numpy as jnp
from jax import lax
from jax.sharding import Mesh
from jax.sharding import PartitionSpec as P

GX = ("gx_0", "gx_1")


def with_halo(array, sides, width):
    for axis, dim in sides:
        devices, length = (lax.axis_size(axis), array.shape[dim])
        up = [(i, (i + 1) % devices) for i in range(devices - 1)]
        down = [(j, i) for i, j in up]
        last = lax.slice_in_dim(array, length - width, length, axis=dim)
        first = lax.slice_in_dim(array, 0, width, axis=dim)
        before = lax.ppermute(last, axis, up)
        after = lax.ppermute(first, axis, down)
        array = jnp.concatenate([before, array, after], axis=dim)
    return array


def sum_by_axis(array, axes, dim):
    for axis in axes:
        array = lax.psum_scatter(array, axis, scatter_dimension=dim, tiled=True)
    return array


def cut_along(array, dim, devices):
    shape = array.shape
    tiles = array.reshape(*shape[:dim], devices, shape[dim] // devices, *shape[dim + 1 :])
    return jnp.moveaxis(tiles, dim, 0)


def sent_and_summed(array, axis, dim):
    devices = lax.axis_size(axis)
    tiles = lax.all_to_all(cut_along(array, dim, devices), axis, 0, 0, tiled=True)
    return jnp.sum(tiles, axis=0)


def offsets():
    return [
        (first, second, third) for first in range(3) for second in range(3) for third in range(3)
    ]


def body(inputs, cotangent, weight, occupancy):
    span_x, span_y, depth, channels = inputs.shape
    count = span_x * span_y * depth
    filled = occupancy.astype(jnp.float32)[..., None]
    masked = inputs * filled
    bordered = with_halo(masked, ((GX, 0), ("gy", 1)), 1)
    padded = jnp.pad(bordered, ((0, 0), (0, 0), (1, 1), (0, 0)))
    preact = jnp.zeros((count, channels), jnp.float32)
    for index, (first, second, third) in enumerate(offsets()):
        piece = padded[
            first : first + span_x, second : second + span_y, third : third + depth
        ].reshape(count, channels)
        preact = preact + jnp.dot(
            piece,
            weight[index * channels : (index + 1) * channels],
            precision=lax.Precision.HIGHEST,
            preferred_element_type=jnp.float32,
        )
    sigma = jax.nn.sigmoid(preact)
    upstream = (
        cotangent.reshape(count, channels)
        * sigma
        * (1.0 + preact * (1.0 - sigma))
        * filled.reshape(count, 1)
    )
    grid_up = upstream.reshape(span_x, span_y, depth, channels)
    border_up = with_halo(grid_up, ((GX, 0), ("gy", 1)), 1)
    border_up = jnp.pad(border_up, ((0, 0), (0, 0), (1, 1), (0, 0)))
    result = jnp.zeros((count, channels), jnp.float32)
    for index, (first, second, third) in enumerate(offsets()):
        kernel = weight[index * channels : (index + 1) * channels]
        back = border_up[
            2 - first : 2 - first + span_x,
            2 - second : 2 - second + span_y,
            2 - third : 2 - third + depth,
        ].reshape(count, channels)
        result = result + jnp.dot(
            back, kernel.T, precision=lax.Precision.HIGHEST, preferred_element_type=jnp.float32
        )
    result = result.reshape(span_x, span_y, depth, channels)
    input_grad = result * filled
    blocks = []
    for index, (first, second, third) in enumerate(offsets()):
        piece = padded[
            first : first + span_x, second : second + span_y, third : third + depth
        ].reshape(count, channels)
        blocks.append(
            jnp.dot(
                piece.T,
                upstream,
                precision=lax.Precision.HIGHEST,
                preferred_element_type=jnp.float32,
            )
        )
    term = jnp.concatenate(blocks, axis=0)
    row_sums = sum_by_axis(term, GX, 0)
    weight_grad = sent_and_summed(row_sums, "gy", 1)
    return (input_grad, weight_grad)


def solution(mesh):
    split = Mesh(mesh.devices.reshape(4, 4, mesh.shape["gy"]), ("gx_0", "gx_1", "gy"))
    in_specs = (P(GX, "gy", None, None), P(GX, "gy", None, None), P(), P(GX, "gy", None))
    out_specs = (P(GX, "gy", None, None), P(GX, "gy"))
    return jax.shard_map(body, mesh=split, in_specs=in_specs, out_specs=out_specs, check_vma=False)
```

profile of v0, /device:TPU:0, one launch (start us, length us, event | category | flops | bytes accessed | tf_op | source)
XLA Modules:
  0.0 325.6 jit_solution(5032757947770603941)
XLA Ops:
  9.4 3.5 %collective-permute-start = (f32[1,8,16,256]{3,2,1,0:T(8,128)S(1)}, f32[1,8,16,256]{3,2,1,0:T(8,128)S(1)}, u32[]{:S(2)}, u32[]{:S(2)}) collective-permute-start(f32[1,8,16,256]{3,2,1,0:T(8,128)S(1)} %get-tuple-element.64), channel_id=1, source_target_pairs={{0,8},{8,16},{16,24},{24,32},{32,40},{40,48},{48,56},{56,64},{64,7... | collective-permute-start | bytes 393224 | tf_op jit(solution)/shard_map/ppermute | solution.py:17
  14.3 3.0 fusion.79
  22.7 3.1 fusion.45
  41.7 6.4 %fusion.134 = (f32[8,8,16,256]{3,2,1,0:T(8,128)}, f32[8,8,16,256]{3,2,1,0:T(8,128)}, f32[8,8,16,256]{3,2,1,0:T(8,128)}, f32[8,8,16,256]{3,2,1,0:T(8,128)}, f32[8...) fusion(f32[10,10,18,256]{3,2,1,0:T(8,128)S(1)} %select_maximum_, ...), kind=kLoop, calls=%fused_computation.190 | loop fusion | bytes 37748736 | tf_op jit(solution)/shard_map/slice | solution.py:56
  48.2 3.6 %fusion.37 = f32[1024,256]{1,0:T(8,128)} fusion(f32[1024,256]{1,0:T(8,128)} %bitcast.190, f32[6912,256]{1,0:T(8,128)S(1)} %copy-done), kind=kOutput, calls=%fused_computation.87 | convolution fusion | flops 805306368 | bytes 2359296 | tf_op jit(solution)/shard_map/dot_general | solution.py:59
  51.8 3.3 %fusion.131 = f32[1024,256]{1,0:T(8,128)} fusion(f32[1024,256]{1,0:T(8,128)} %bitcast.226, f32[6912,256]{1,0:T(8,128)S(1)} %copy-done), kind=kOutput, calls=%fused_computation.181 | convolution fusion | flops 805306368 | bytes 2359296 | tf_op jit(solution)/shard_map/dot_general | solution.py:59
  55.1 3.3 fusion.41
  74.1 15.1 %fusion.99 = f32[1024,256]{1,0:T(8,128)} fusion(f32[1024,256]{1,0:T(8,128)S(1)} %bitcast.216, f32[6912,256]{1,0:T(8,128)S(1)} %copy-done), kind=kOutput, calls=%fused_computation.149 | convolution fusion | flops 805306368 | bytes 2359296 | tf_op jit(solution)/shard_map/dot_general | solution.py:59
  99.0 10.3 %fusion.26 = f32[1024,256]{1,0:T(8,128)S(1)} fusion(f32[8,8,16,256]{3,2,1,0:T(8,128)} %param.5, f32[1024,256]{1,0:T(8,128)} %fusion.29, f32[1024,256]{1,0:T(8,128)} %fusion.33, f32[1024,256]{1,0:T(8,128)} %fusion.37, f32[1024,256]{1,0:T(8,128)} %fusion.41, f32[1024,256]{1,0:T(8,128)} %fusion.45, f32[1024,256]{1,0:T(8,128)} %fusion.49, ...), kind=kOutput, calls=%fused_computation.74 | convolution fusion | flops 814481408 | bytes 30674944 | tf_op jit(solution)/shard_map/dot_general | solution.py:59
  114.6 3.8 %convolution_dynamic-update-slice_fusion.24 = f32[6912,256]{1,0:T(8,128)} fusion(f32[6912,256]{1,0:T(8,128)} %convolution_dynamic-update-slice_fusion.25, f32[1024,256]{1,0:T(8,128)} %bitcast.224, f32[1024,256]{1,0:T(8,128)S(1)} %fusion.26), kind=kOutput, calls=%fused_computation.65 | convolution fusion | flops 805306368 | bytes 2359296 | tf_op jit(solution)/shard_map/dot_general | solution.py:94
  126.0 2.9 convolution_dynamic-update-slice_fusion.20
  128.9 2.6 convolution_dynamic-update-slice_fusion.19
  141.7 2.6 convolution_dynamic-update-slice_fusion.14
  144.3 2.7 convolution_dynamic-update-slice_fusion.13
  162.4 2.8 convolution_dynamic-update-slice_fusion.6
  165.2 2.6 convolution_dynamic-update-slice_fusion.5
  167.8 2.6 convolution_dynamic-update-slice_fusion.4
  182.3 4.6 %collective-permute-start.4 = (f32[1,8,16,256]{3,2,1,0:T(8,128)S(1)}, f32[1,8,16,256]{3,2,1,0:T(8,128)S(1)}, u32[]{:S(2)}, u32[]{:S(2)}) collective-permute-start(f32[1,8,16,256]{3,2,1,0:T(8,128)S(1)} %bitcast.260), channel_id=1, source_target_pairs={{0,8},{8,16},{16,24},{24,32},{32,40},{40,48},{48,56},{56,64},{64,7... | collective-permute-start | bytes 393224 | tf_op jit(solution)/shard_map/ppermute | solution.py:17
  189.4 3.8 %collective-permute-start.6 = (f32[10,1,16,256]{3,2,1,0:T(8,128)S(1)}, f32[10,1,16,256]{3,2,1,0:T(8,128)S(1)}, u32[]{:S(2)}, u32[]{:S(2)}) collective-permute-start(f32[10,1,16,256]{3,2,1,0:T(8,128)S(1)} %get-tuple-element.52), channel_id=1, source_target_pairs={{0,1},{1,2},{2,3},{3,4},{4,5},{5,6},{6,7},{8,9},{9,10},{10,11},{11... | collective-permute-start | bytes 491528 | tf_op jit(solution)/shard_map/ppermute | solution.py:17
  194.7 2.9 fusion.113
  197.7 3.0 fusion.43
  201.5 3.0 fusion.125
  204.5 3.0 fusion.55
  207.4 2.9 fusion.89
  210.8 3.0 fusion.101
  213.8 3.0 fusion.31
  216.7 3.0 fusion.67
  220.2 5.3 %fusion.133 = (f32[8,8,16,256]{3,2,1,0:T(8,128)S(1)}, f32[8,8,16,256]{3,2,1,0:T(8,128)S(1)}, f32[8,8,16,256]{3,2,1,0:T(8,128)S(1)}, f32[8,8,16,256]{3,2,1,0:T(8,...) fusion(f32[10,10,18,256]{3,2,1,0:T(8,128)S(1)} %select_maximum_, ...), kind=kLoop, calls=%fused_computation.189 | loop fusion | bytes 37748736 | tf_op jit(solution)/shard_map/slice | solution.py:78
  225.5 3.0 fusion.129
  228.5 2.9 fusion.35
  231.5 3.0 fusion.39
  234.5 2.9 fusion.47
  237.4 21.0 %reduce-scatter.3.cloned.1.call-done = f32[1728,256]{1,0:T(8,128)} async-done(((f32[6912,256]{1,0:T(8,128)}), f32[1728,256]{1,0:T(8,128)}) %reduce-scatter.3.cloned.1.call-update) | async-done | bytes 1769488 | tf_op jit(solution)/shard_map/reduce_scatter | solution.py:25
  258.4 3.5 %fusion.51 = f32[1024,256]{1,0:T(8,128)} fusion(f32[1024,256]{1,0:T(8,128)} %bitcast.245, f32[6912,256]{1,0:T(8,128)} %param.6), kind=kOutput, calls=%fused_computation.101 | convolution fusion | flops 805306368 | bytes 2359296 | tf_op jit(solution)/shard_map/dot_general | solution.py:83
  261.9 3.3 %fusion.59 = f32[1024,256]{1,0:T(8,128)} fusion(f32[1024,256]{1,0:T(8,128)} %bitcast.244, f32[6912,256]{1,0:T(8,128)} %param.6), kind=kOutput, calls=%fused_computation.109 | convolution fusion | flops 805306368 | bytes 2359296 | tf_op jit(solution)/shard_map/dot_general | solution.py:83
  265.2 3.4 %fusion.63 = f32[1024,256]{1,0:T(8,128)} fusion(f32[1024,256]{1,0:T(8,128)} %bitcast.243, f32[6912,256]{1,0:T(8,128)} %param.6), kind=kOutput, calls=%fused_computation.113 | convolution fusion | flops 805306368 | bytes 2359296 | tf_op jit(solution)/shard_map/dot_general | solution.py:83
  268.5 3.1 fusion.71
  271.6 3.1 fusion.81
  274.7 3.1 fusion.85
  277.8 3.0 fusion.93
  280.8 3.2 fusion.97
  284.0 3.1 fusion.105
  287.1 3.0 fusion.109
  290.1 3.0 fusion.117
  293.1 3.0 fusion.121
  296.1 2.9 fusion.27
  301.0 4.3 %all-to-all-start = ((f32[8,432,32]{1,2,0:T(8,128)}), f32[8,432,32]{1,2,0:T(8,128)}, u32[]{:S(2)}, u32[]{:S(2)}) async-start(f32[8,432,32]{1,2,0:T(8,128)} %bitcast.259), calls=%async_computation.2 | async-start | bytes 1048576 | tf_op jit(solution)/shard_map/all_to_all | solution.py:37
  305.4 10.3 %fusion.23 = f32[1024,256]{1,0:T(8,128)S(1)} fusion(f32[1024,256]{1,0:T(8,128)} %fusion.27, f32[1024,256]{1,0:T(8,128)} %fusion.31, f32[1024,256]{1,0:T(8,128)} %fusion.35, f32[1024,256]{1,0:T(8,128)} %fusion.39, f32[1024,256]{1,0:T(8,128)} %fusion.43, f32[1024,256]{1,0:T(8,128)} %fusion.47, f32[1024,256]{1,0:T(8,128)} %fusion.51, f32[1024,256]{1,0:T(8,128)} %fusion.55, ...), kind=kOutput, calls=%fused_computation.39 | convolution fusion | flops 812122112 | bytes 29622272 | tf_op jit(solution)/shard_map/dot_general | solution.py:83
  (180 shorter events, 111.2 us)
Async XLA Ops:
  7.2 251.2 %reduce-scatter.3.cloned.1.call-start = ((), (), s32[]{:S(2)}) async-start(), calls=%async_computation.3 | async-start | bytes 8847360 | tf_op jit(solution)/shard_map/reduce_scatter | solution.py:25
  9.4 7.9 %collective-permute-start = (f32[1,8,16,256]{3,2,1,0:T(8,128)S(1)}, f32[1,8,16,256]{3,2,1,0:T(8,128)S(1)}, u32[]{:S(2)}, u32[]{:S(2)}) collective-permute-start(f32[1,8,16,256]{3,2,1,0:T(8,128)S(1)} %get-tuple-element.64), channel_id=1, source_target_pairs={{0,8},{8,16},{16,24},{24,32},{32,40},{40,48},{48,56},{56,64},{64,7... | collective-permute-start | bytes 393224 | tf_op jit(solution)/shard_map/ppermute | solution.py:17
  13.0 6.9 %collective-permute-start.1 = (f32[1,8,16,256]{3,2,1,0:T(8,128)S(1)}, f32[1,8,16,256]{3,2,1,0:T(8,128)S(1)}, u32[]{:S(2)}, u32[]{:S(2)}) collective-permute-start(f32[1,8,16,256]{3,2,1,0:T(8,128)S(1)} %get-tuple-element.65), channel_id=1, source_target_pairs={{8,0},{16,8},{24,16},{32,24},{40,32},{48,40},{56,48},{64,56},{72,6... | collective-permute-start | bytes 393224 | tf_op jit(solution)/shard_map/ppermute | solution.py:18
  19.8 8.0 %collective-permute-start.2 = (f32[10,1,16,256]{3,2,1,0:T(8,128)S(1)}, f32[10,1,16,256]{3,2,1,0:T(8,128)S(1)}, u32[]{:S(2)}, u32[]{:S(2)}) collective-permute-start(f32[10,1,16,256]{3,2,1,0:T(8,128)S(1)} %get-tuple-element.56), channel_id=1, source_target_pairs={{0,1},{1,2},{2,3},{3,4},{4,5},{5,6},{6,7},{8,9},{9,10},{10,11},{11... | collective-permute-start | bytes 491528 | tf_op jit(solution)/shard_map/ppermute | solution.py:17
  21.1 6.7 %collective-permute-start.3 = (f32[10,1,16,256]{3,2,1,0:T(8,128)S(1)}, f32[10,1,16,256]{3,2,1,0:T(8,128)S(1)}, u32[]{:S(2)}, u32[]{:S(2)}) collective-permute-start(f32[10,1,16,256]{3,2,1,0:T(8,128)S(1)} %get-tuple-element.57), channel_id=1, source_target_pairs={{1,0},{2,1},{3,2},{4,3},{5,4},{6,5},{7,6},{9,8},{10,9},{11,10},{12... | collective-permute-start | bytes 491528 | tf_op jit(solution)/shard_map/ppermute | solution.py:18
  28.9 12.4 %copy-start.1 = (f32[8,8,16,256]{3,2,1,0:T(8,128)}, f32[8,8,16,256]{3,2,1,0:T(8,128)S(1)}, u32[]{:S(2)}) copy-start(f32[8,8,16,256]{3,2,1,0:T(8,128)S(1)} %get-tuple-element.45) | copy-start | bytes 3145732
  28.9 12.4 %copy-start.3 = (f32[8,8,16,256]{3,2,1,0:T(8,128)}, f32[8,8,16,256]{3,2,1,0:T(8,128)S(1)}, u32[]{:S(2)}) copy-start(f32[8,8,16,256]{3,2,1,0:T(8,128)S(1)} %get-tuple-element.66) | copy-start | bytes 3145732
  28.9 12.4 %copy-start.9 = (f32[8,8,16,256]{3,2,1,0:T(8,128)}, f32[8,8,16,256]{3,2,1,0:T(8,128)S(1)}, u32[]{:S(2)}) copy-start(f32[8,8,16,256]{3,2,1,0:T(8,128)S(1)} %get-tuple-element.46) | copy-start | bytes 3145732
  28.9 12.4 %copy-start.14 = (f32[8,8,16,256]{3,2,1,0:T(8,128)}, f32[8,8,16,256]{3,2,1,0:T(8,128)S(1)}, u32[]{:S(2)}) copy-start(f32[8,8,16,256]{3,2,1,0:T(8,128)S(1)} %get-tuple-element.68) | copy-start | bytes 3145732
  28.9 12.4 %copy-start.20 = (f32[8,8,16,256]{3,2,1,0:T(8,128)}, f32[8,8,16,256]{3,2,1,0:T(8,128)S(1)}, u32[]{:S(2)}) copy-start(f32[8,8,16,256]{3,2,1,0:T(8,128)S(1)} %get-tuple-element.44) | copy-start | bytes 3145732
  28.9 12.4 %copy-start.48 = (f32[1,8,16,256]{3,2,1,0:T(8,128)S(1)}, f32[1,8,16,256]{3,2,1,0:T(8,128)}, u32[]{:S(2)}) copy-start(f32[1,8,16,256]{3,2,1,0:T(8,128)} %copy-done.47) | copy-start | bytes 393220
  28.9 12.4 %copy-start.50 = (f32[1,8,16,256]{3,2,1,0:T(8,128)S(1)}, f32[1,8,16,256]{3,2,1,0:T(8,128)}, u32[]{:S(2)}) copy-start(f32[1,8,16,256]{3,2,1,0:T(8,128)} %copy-done.49) | copy-start | bytes 393220
  48.1 48.9 %copy-start.5 = (f32[8,8,16,256]{3,2,1,0:T(8,128)}, f32[8,8,16,256]{3,2,1,0:T(8,128)S(1)}, u32[]{:S(2)}) copy-start(f32[8,8,16,256]{3,2,1,0:T(8,128)S(1)} %get-tuple-element.37) | copy-start | bytes 3145732
  48.2 14.1 %copy-start.13 = (f32[8,8,16,256]{3,2,1,0:T(8,128)S(1)}, f32[8,8,16,256]{3,2,1,0:T(8,128)}, u32[]{:S(2)}) copy-start(f32[8,8,16,256]{3,2,1,0:T(8,128)} %get-tuple-element.25) | copy-start | bytes 3145732
  48.2 16.1 %copy-start.16 = (f32[8,8,16,256]{3,2,1,0:T(8,128)S(1)}, f32[8,8,16,256]{3,2,1,0:T(8,128)}, u32[]{:S(2)}) copy-start(f32[8,8,16,256]{3,2,1,0:T(8,128)} %get-tuple-element.26) | copy-start | bytes 3145732
  51.7 14.5 %copy-start.17 = (f32[8,8,16,256]{3,2,1,0:T(8,128)S(1)}, f32[8,8,16,256]{3,2,1,0:T(8,128)}, u32[]{:S(2)}) copy-start(f32[8,8,16,256]{3,2,1,0:T(8,128)} %get-tuple-element.27) | copy-start | bytes 3145732
  55.1 13.1 %copy-start.18 = (f32[8,8,16,256]{3,2,1,0:T(8,128)S(1)}, f32[8,8,16,256]{3,2,1,0:T(8,128)}, u32[]{:S(2)}) copy-start(f32[8,8,16,256]{3,2,1,0:T(8,128)} %get-tuple-element.29) | copy-start | bytes 3145732
  64.3 24.9 %copy-start.25 = (f32[8,8,16,256]{3,2,1,0:T(8,128)S(1)}, f32[8,8,16,256]{3,2,1,0:T(8,128)}, u32[]{:S(2)}) copy-start(f32[8,8,16,256]{3,2,1,0:T(8,128)} %get-tuple-element.33) | copy-start | bytes 3145732
  66.2 24.9 %copy-start.27 = (f32[8,8,16,256]{3,2,1,0:T(8,128)S(1)}, f32[8,8,16,256]{3,2,1,0:T(8,128)}, u32[]{:S(2)}) copy-start(f32[8,8,16,256]{3,2,1,0:T(8,128)} %get-tuple-element.34) | copy-start | bytes 3145732
  68.2 24.9 %copy-start.29 = (f32[8,8,16,256]{3,2,1,0:T(8,128)S(1)}, f32[8,8,16,256]{3,2,1,0:T(8,128)}, u32[]{:S(2)}) copy-start(f32[8,8,16,256]{3,2,1,0:T(8,128)} %get-tuple-element.35) | copy-start | bytes 3145732
  70.2 24.9 %copy-start.31 = (f32[8,8,16,256]{3,2,1,0:T(8,128)S(1)}, f32[8,8,16,256]{3,2,1,0:T(8,128)}, u32[]{:S(2)}) copy-start(f32[8,8,16,256]{3,2,1,0:T(8,128)} %get-tuple-element.36) | copy-start | bytes 3145732
  99.0 13.0 %copy-start.21 = (f32[8,8,16,256]{3,2,1,0:T(8,128)S(1)}, f32[8,8,16,256]{3,2,1,0:T(8,128)}, u32[]{:S(2)}) copy-start(f32[8,8,16,256]{3,2,1,0:T(8,128)} %copy-done.20) | copy-start | bytes 3145732
  109.4 14.1 %copy-start.28 = (f32[8,8,16,256]{3,2,1,0:T(8,128)S(1)}, f32[8,8,16,256]{3,2,1,0:T(8,128)}, u32[]{:S(2)}) copy-start(f32[8,8,16,256]{3,2,1,0:T(8,128)} %get-tuple-element.34) | copy-start | bytes 3145732
  109.4 16.6 %copy-start.26 = (f32[8,8,16,256]{3,2,1,0:T(8,128)S(1)}, f32[8,8,16,256]{3,2,1,0:T(8,128)}, u32[]{:S(2)}) copy-start(f32[8,8,16,256]{3,2,1,0:T(8,128)} %get-tuple-element.33) | copy-start | bytes 3145732
  112.0 16.9 %copy-start.15 = (f32[8,8,16,256]{3,2,1,0:T(8,128)S(1)}, f32[8,8,16,256]{3,2,1,0:T(8,128)}, u32[]{:S(2)}) copy-start(f32[8,8,16,256]{3,2,1,0:T(8,128)} %copy-done.14) | copy-start | bytes 3145732
  114.6 17.0 %copy-start.24 = (f32[8,8,16,256]{3,2,1,0:T(8,128)S(1)}, f32[8,8,16,256]{3,2,1,0:T(8,128)}, u32[]{:S(2)}) copy-start(f32[8,8,16,256]{3,2,1,0:T(8,128)} %get-tuple-element.32) | copy-start | bytes 3145732
  120.9 15.7 %copy-start.10 = (f32[8,8,16,256]{3,2,1,0:T(8,128)S(1)}, f32[8,8,16,256]{3,2,1,0:T(8,128)}, u32[]{:S(2)}) copy-start(f32[8,8,16,256]{3,2,1,0:T(8,128)} %copy-done.9) | copy-start | bytes 3145732
  136.7 15.5 %copy-start.4 = (f32[8,8,16,256]{3,2,1,0:T(8,128)S(1)}, f32[8,8,16,256]{3,2,1,0:T(8,128)}, u32[]{:S(2)}) copy-start(f32[8,8,16,256]{3,2,1,0:T(8,128)} %copy-done.3) | copy-start | bytes 3145732
  144.3 15.6 %copy-start.2 = (f32[8,8,16,256]{3,2,1,0:T(8,128)S(1)}, f32[8,8,16,256]{3,2,1,0:T(8,128)}, u32[]{:S(2)}) copy-start(f32[8,8,16,256]{3,2,1,0:T(8,128)} %copy-done.1) | copy-start | bytes 3145732
  152.2 15.6 %copy-start.34 = (f32[8,8,16,256]{3,2,1,0:T(8,128)S(1)}, f32[8,8,16,256]{3,2,1,0:T(8,128)}, u32[]{:S(2)}) copy-start(f32[8,8,16,256]{3,2,1,0:T(8,128)} %copy-done.33) | copy-start | bytes 3145732
  154.7 15.7 %copy-start.8 = (f32[8,8,16,256]{3,2,1,0:T(8,128)S(1)}, f32[8,8,16,256]{3,2,1,0:T(8,128)}, u32[]{:S(2)}) copy-start(f32[8,8,16,256]{3,2,1,0:T(8,128)} %get-tuple-element.22) | copy-start | bytes 3145732
  157.3 15.6 %copy-start.7 = (f32[8,8,16,256]{3,2,1,0:T(8,128)S(1)}, f32[8,8,16,256]{3,2,1,0:T(8,128)}, u32[]{:S(2)}) copy-start(f32[8,8,16,256]{3,2,1,0:T(8,128)} %get-tuple-element.21) | copy-start | bytes 3145732
  162.4 15.6 %copy-start.6 = (f32[8,8,16,256]{3,2,1,0:T(8,128)S(1)}, f32[8,8,16,256]{3,2,1,0:T(8,128)}, u32[]{:S(2)}) copy-start(f32[8,8,16,256]{3,2,1,0:T(8,128)} %copy-done.5) | copy-start | bytes 3145732
  180.5 118.5 %reduce-scatter.5.cloned.1.call-start = ((), (), s32[]{:S(2)}) async-start(), calls=%async_computation.4 | async-start | bytes 2211840 | tf_op jit(solution)/shard_map/reduce_scatter | solution.py:25
  181.0 7.8 %collective-permute-start.5 = (f32[1,8,16,256]{3,2,1,0:T(8,128)S(1)}, f32[1,8,16,256]{3,2,1,0:T(8,128)S(1)}, u32[]{:S(2)}, u32[]{:S(2)}) collective-permute-start(f32[1,8,16,256]{3,2,1,0:T(8,128)S(1)} %bitcast.261), channel_id=1, source_target_pairs={{8,0},{16,8},{24,16},{32,24},{40,32},{48,40},{56,48},{64,56},{72,6... | collective-permute-start | bytes 393224 | tf_op jit(solution)/shard_map/ppermute | solution.py:18
  182.3 7.1 %collective-permute-start.4 = (f32[1,8,16,256]{3,2,1,0:T(8,128)S(1)}, f32[1,8,16,256]{3,2,1,0:T(8,128)S(1)}, u32[]{:S(2)}, u32[]{:S(2)}) collective-permute-start(f32[1,8,16,256]{3,2,1,0:T(8,128)S(1)} %bitcast.260), channel_id=1, source_target_pairs={{0,8},{8,16},{16,24},{24,32},{32,40},{40,48},{48,56},{56,64},{64,7... | collective-permute-start | bytes 393224 | tf_op jit(solution)/shard_map/ppermute | solution.py:17
  189.4 11.3 %collective-permute-start.6 = (f32[10,1,16,256]{3,2,1,0:T(8,128)S(1)}, f32[10,1,16,256]{3,2,1,0:T(8,128)S(1)}, u32[]{:S(2)}, u32[]{:S(2)}) collective-permute-start(f32[10,1,16,256]{3,2,1,0:T(8,128)S(1)} %get-tuple-element.52), channel_id=1, source_target_pairs={{0,1},{1,2},{2,3},{3,4},{4,5},{5,6},{6,7},{8,9},{9,10},{10,11},{11... | collective-permute-start | bytes 491528 | tf_op jit(solution)/shard_map/ppermute | solution.py:17
  193.2 7.5 %collective-permute-start.7 = (f32[10,1,16,256]{3,2,1,0:T(8,128)S(1)}, f32[10,1,16,256]{3,2,1,0:T(8,128)S(1)}, u32[]{:S(2)}, u32[]{:S(2)}) collective-permute-start(f32[10,1,16,256]{3,2,1,0:T(8,128)S(1)} %get-tuple-element.53), channel_id=1, source_target_pairs={{1,0},{2,1},{3,2},{4,3},{5,4},{6,5},{7,6},{9,8},{10,9},{11,10},{12... | collective-permute-start | bytes 491528 | tf_op jit(solution)/shard_map/ppermute | solution.py:18
  258.4 13.2 %copy-start.45 = (f32[8,8,16,256]{3,2,1,0:T(8,128)S(1)}, f32[8,8,16,256]{3,2,1,0:T(8,128)}, u32[]{:S(2)}) copy-start(f32[8,8,16,256]{3,2,1,0:T(8,128)} %get-tuple-element.11) | copy-start | bytes 3145732
  258.4 16.3 %copy-start.44 = (f32[8,8,16,256]{3,2,1,0:T(8,128)S(1)}, f32[8,8,16,256]{3,2,1,0:T(8,128)}, u32[]{:S(2)}) copy-start(f32[8,8,16,256]{3,2,1,0:T(8,128)} %get-tuple-element.12) | copy-start | bytes 3145732
  258.4 19.3 %copy-start.43 = (f32[8,8,16,256]{3,2,1,0:T(8,128)S(1)}, f32[8,8,16,256]{3,2,1,0:T(8,128)}, u32[]{:S(2)}) copy-start(f32[8,8,16,256]{3,2,1,0:T(8,128)} %get-tuple-element.13) | copy-start | bytes 3145732
  265.2 18.8 %copy-start.42 = (f32[8,8,16,256]{3,2,1,0:T(8,128)S(1)}, f32[8,8,16,256]{3,2,1,0:T(8,128)}, u32[]{:S(2)}) copy-start(f32[8,8,16,256]{3,2,1,0:T(8,128)} %get-tuple-element.15) | copy-start | bytes 3145732
  268.5 18.6 %copy-start.41 = (f32[8,8,16,256]{3,2,1,0:T(8,128)S(1)}, f32[8,8,16,256]{3,2,1,0:T(8,128)}, u32[]{:S(2)}) copy-start(f32[8,8,16,256]{3,2,1,0:T(8,128)} %get-tuple-element.16) | copy-start | bytes 3145732
  271.6 18.5 %copy-start.40 = (f32[8,8,16,256]{3,2,1,0:T(8,128)S(1)}, f32[8,8,16,256]{3,2,1,0:T(8,128)}, u32[]{:S(2)}) copy-start(f32[8,8,16,256]{3,2,1,0:T(8,128)} %get-tuple-element.17) | copy-start | bytes 3145732
  274.7 18.4 %copy-start.39 = (f32[8,8,16,256]{3,2,1,0:T(8,128)S(1)}, f32[8,8,16,256]{3,2,1,0:T(8,128)}, u32[]{:S(2)}) copy-start(f32[8,8,16,256]{3,2,1,0:T(8,128)} %get-tuple-element.18) | copy-start | bytes 3145732
  277.8 18.3 %copy-start.38 = (f32[8,8,16,256]{3,2,1,0:T(8,128)S(1)}, f32[8,8,16,256]{3,2,1,0:T(8,128)}, u32[]{:S(2)}) copy-start(f32[8,8,16,256]{3,2,1,0:T(8,128)} %get-tuple-element.19) | copy-start | bytes 3145732
  284.0 21.4 %copy-start.37 = (f32[1024,256]{1,0:T(8,128)S(1)}, f32[1024,256]{1,0:T(8,128)}, u32[]{:S(2)}) copy-start(f32[1024,256]{1,0:T(8,128)} %fusion.113) | copy-start | bytes 3145732
  301.0 15.8 %all-to-all-start = ((f32[8,432,32]{1,2,0:T(8,128)}), f32[8,432,32]{1,2,0:T(8,128)}, u32[]{:S(2)}, u32[]{:S(2)}) async-start(f32[8,432,32]{1,2,0:T(8,128)} %bitcast.259), calls=%async_computation.2 | async-start | bytes 1048576 | tf_op jit(solution)/shard_map/all_to_all | solution.py:37
  (14 other events, 138.0 us)
Sparse Core Ops, SparseCore 0:
  180.6 77.6 reduce-scatter.2
  260.8 26.5 reduce-scatter.4
where the time goes:
time: 331 us; the launch traced here: 326 us
  matrix products  241 us (73%)
  waiting for transfers between devices  24 us (7%)
  starting transfers between devices  23.1 us (7%)
  local copies, waits for them, and re-layouts  15.4 us (5%)
  between operations  14.8 us (4%)
  other arithmetic  7.33 us (2%)
    dot_general x27, matrix products, body(): jnp.dot(back, kernel.T, precision=lax.Precision.HIGHEST, preferred_elemen...  88.4 us
    dot_general x27, matrix products, body(): jnp.dot(piece, weight[index * channels:(index + 1) * channels], precision...  81.5 us
    dot_general x27, matrix products, body(): jnp.dot(piece.T, upstream, precision=lax.Precision.HIGHEST, preferred_ele...  71 us
    reduce_scatter x2, waiting for transfers between devices, sum_by_axis(): array = lax.psum_scatter(array, axis, scatter_dimension=dim, tiled=True)  21 us
    ppermute x4, starting transfers between devices, with_halo(): before = lax.ppermute(last, axis, up)  13.2 us
    slice x2, local copies, waits for them, and re-layouts, body(): padded[first:first + span_x, second:second + span_y, third:third + depth]  6.93 us
  transfers between devices with their start and end apart: 11, of which 3 were waited for; matrix products, arithmetic and copies ran while one was open for 32% of the time, Pallas kernels for 0%

commit v1 on v0

v1 whole, which is shorter than its diff:
```python
import jax, jax.numpy as jnp
from jax import lax
from jax.experimental import pallas as pl
from jax.experimental.pallas import tpu as pltpu
from jax.sharding import Mesh
from jax.sharding import PartitionSpec as P

GX = ("gx_0", "gx_1")
F32 = jnp.float32
BF16 = jnp.bfloat16


def split(value):
    high = value.astype(BF16)
    return high, (value - high.astype(F32)).astype(BF16)


def rows(index, size):
    return pl.ds(pl.multiple_of(index * size, size), size)


def filter_points(a, b, c):
    outer, inner = (a + c) * 0.5, b * 0.5
    return a, outer + inner, outer - inner, c


def data_points(a, b, c, d):
    return a - c, b + c, c - b, b - d


def sums_of_points(a, b, c, d):
    return a + b + c, b - c - d


def points_of_pair(a, b):
    return a, a + b, a - b, -b


def taps_of_points(a, b, c, d):
    outer = (b + c) * 0.5
    return a + outer, (b - c) * 0.5, outer + d


def both(function, grid):
    half = list(zip(*[function(*column) for column in zip(*grid)]))
    return [function(*row) for row in half]


def transform_weight(weight, high, low):
    def step(index, carry):
        grid = [
            [weight[pl.ds(pl.multiple_of((3 * a + b) * 768 + index * 16, 16), 16)] for b in range(3)]
            for a in range(3)
        ]
        points = both(filter_points, grid)
        for u in range(4):
            for v in range(4):
                top, rest = split(points[u][v])
                high[4 * u + v, rows(index, 16)] = top
                low[4 * u + v, rows(index, 16)] = rest
        return carry

    lax.fori_loop(0, 48, step, 0)


def transform_data(padded, high, low):
    def step(tile, carry):
        x, y = tile // 4, tile % 4
        grid = [[padded[2 * x + i, 2 * y + j] for j in range(4)] for i in range(4)]
        points = both(data_points, grid)
        zero = jnp.zeros((1, 256), F32)
        for u in range(4):
            for v in range(4):
                mid = points[u][v]
                down = jnp.concatenate([zero, mid[:15]], axis=0)
                up = jnp.concatenate([mid[1:], zero], axis=0)
                for place, piece in enumerate((down, mid, up)):
                    top, rest = split(piece)
                    high[4 * u + v, rows(tile, 16), 256 * place : 256 * place + 256] = top
                    low[4 * u + v, rows(tile, 16), 256 * place : 256 * place + 256] = rest
        return carry

    lax.fori_loop(0, 16, step, 0)


def dots(left_high, left_low, right_high, right_low, numbers):
    dims = (numbers, ((), ()))
    return (
        lax.dot_general(left_high, right_high, dims, preferred_element_type=F32)
        + lax.dot_general(left_low, right_high, dims, preferred_element_type=F32)
        + lax.dot_general(left_high, right_low, dims, preferred_element_type=F32)
    )


def forward(data_high, data_low, filter_high, filter_low, product):
    def step(point, carry):
        product[point] = dots(
            data_high[point], data_low[point], filter_high[point], filter_low[point], ((1,), (0,))
        )
        return carry

    lax.fori_loop(0, 16, step, 0)


def backward(data_high, data_low, filter_high, filter_low, product):
    def step(point, carry):
        u, v = point // 4, point % 4
        u = jnp.where(u == 0, 3, jnp.where(u == 3, 0, u))
        v = jnp.where(v == 0, 3, jnp.where(v == 3, 0, v))
        other = 4 * u + v
        total = None
        for place in range(3):
            lanes = slice(256 * place, 256 * place + 256)
            taps = slice(256 * (2 - place), 256 * (2 - place) + 256)
            term = dots(
                data_high[point, :, lanes],
                data_low[point, :, lanes],
                filter_high[other, taps],
                filter_low[other, taps],
                ((1,), (1,)),
            )
            total = term if total is None else total + term
        product[point] = total
        return carry

    lax.fori_loop(0, 16, step, 0)


def upstream_of(product, cotangent, filled, grid_up, up_high, up_low):
    def step(tile, carry):
        x, y = tile // 4, tile % 4
        grid = [[product[4 * u + v, rows(tile, 16)] for v in range(4)] for u in range(4)]
        sums = both(sums_of_points, grid)
        pair = []
        for i in range(2):
            line = []
            for j in range(2):
                value = sums[i][j]
                sigma = 1.0 / (1.0 + jnp.exp(-value))
                fill = filled[2 * x + i, 2 * y + j]
                fill = jnp.concatenate([fill, fill], axis=1)
                result = cotangent[2 * x + i, 2 * y + j] * sigma * (1.0 + value * (1.0 - sigma)) * fill
                grid_up[2 * x + i, 2 * y + j] = result
                line.append(result)
            pair.append(line)
        points = both(points_of_pair, pair)
        for u in range(4):
            for v in range(4):
                top, rest = split(points[u][v])
                up_high[4 * u + v, rows(tile, 16)] = top
                up_low[4 * u + v, rows(tile, 16)] = rest
        return carry

    lax.fori_loop(0, 16, step, 0)


def weight_terms(data_high, data_low, up_high, up_low, product, term):
    for place in range(3):
        lanes = slice(256 * place, 256 * place + 256)

        def step(point, carry):
            product[point] = dots(
                data_high[point, :, lanes], data_low[point, :, lanes], up_high[point], up_low[point], ((0,), (0,))
            )
            return carry

        lax.fori_loop(0, 16, step, 0)

        def gather(index, carry):
            grid = [[product[4 * u + v, rows(index, 16)] for v in range(4)] for u in range(4)]
            taps = both(taps_of_points, grid)
            for a in range(3):
                for b in range(3):
                    start = (3 * a + b) * 768 + 256 * place
                    term[pl.ds(pl.multiple_of(start + index * 16, 16), 16)] = taps[a][b]
            return carry

        lax.fori_loop(0, 16, gather, 0)


def result_of(product, filled, result):
    def step(tile, carry):
        x, y = tile // 4, tile % 4
        grid = [[product[4 * u + v, rows(tile, 16)] for v in range(4)] for u in range(4)]
        sums = both(sums_of_points, grid)
        for i in range(2):
            for j in range(2):
                fill = filled[2 * x + i, 2 * y + j]
                result[2 * x + i, 2 * y + j] = sums[i][j] * jnp.concatenate([fill, fill], axis=1)
        return carry

    lax.fori_loop(0, 16, step, 0)


def first_kernel(padded, cotangent, filled, weight, grid_up, term, dh, dl, fh, fl, eh, el, product):
    transform_weight(weight, fh, fl)
    transform_data(padded, dh, dl)
    forward(dh, dl, fh, fl, product)
    upstream_of(product, cotangent, filled, grid_up, eh, el)
    weight_terms(dh, dl, eh, el, product, term)


def second_kernel(padded, filled, weight, result, dh, dl, fh, fl, product):
    transform_weight(weight, fh, fl)
    transform_data(padded, dh, dl)
    backward(dh, dl, fh, fl, product)
    result_of(product, filled, result)


IN_VMEM = pl.BlockSpec(memory_space=pltpu.VMEM)
PARAMS = pltpu.CompilerParams(vmem_limit_bytes=63 << 20)
DATA = [pltpu.VMEM((16, 256, 768), BF16)] * 2
FILTER = [pltpu.VMEM((16, 768, 256), BF16)] * 2
PRODUCT = [pltpu.VMEM((16, 256, 256), F32)]


def run_first(padded, cotangent, filled, weight):
    return pl.pallas_call(
        first_kernel,
        out_shape=(jax.ShapeDtypeStruct((8, 8, 16, 256), F32), jax.ShapeDtypeStruct((6912, 256), F32)),
        in_specs=[IN_VMEM] * 4,
        out_specs=(IN_VMEM, IN_VMEM),
        scratch_shapes=DATA + FILTER + [pltpu.VMEM((16, 256, 256), BF16)] * 2 + PRODUCT,
        compiler_params=PARAMS,
        name="first",
    )(padded, cotangent, filled, weight)


def run_second(padded, filled, weight):
    return pl.pallas_call(
        second_kernel,
        out_shape=jax.ShapeDtypeStruct((8, 8, 16, 256), F32),
        in_specs=[IN_VMEM] * 3,
        out_specs=IN_VMEM,
        scratch_shapes=DATA + FILTER + PRODUCT,
        compiler_params=PARAMS,
        name="second",
    )(padded, filled, weight)


def with_halo(array, sides, width):
    for axis, dim in sides:
        devices, length = (lax.axis_size(axis), array.shape[dim])
        up = [(i, (i + 1) % devices) for i in range(devices - 1)]
        down = [(j, i) for i, j in up]
        last = lax.slice_in_dim(array, length - width, length, axis=dim)
        first = lax.slice_in_dim(array, 0, width, axis=dim)
        before = lax.ppermute(last, axis, up)
        after = lax.ppermute(first, axis, down)
        array = jnp.concatenate([before, array, after], axis=dim)
    return array


def sum_by_axis(array, axes, dim):
    for axis in axes:
        array = lax.psum_scatter(array, axis, scatter_dimension=dim, tiled=True)
    return array


def cut_along(array, dim, devices):
    shape = array.shape
    tiles = array.reshape(*shape[:dim], devices, shape[dim] // devices, *shape[dim + 1 :])
    return jnp.moveaxis(tiles, dim, 0)


def sent_and_summed(array, axis, dim):
    devices = lax.axis_size(axis)
    tiles = lax.all_to_all(cut_along(array, dim, devices), axis, 0, 0, tiled=True)
    return jnp.sum(tiles, axis=0)


def body(inputs, cotangent, weight, occupancy):
    filled = occupancy.astype(F32)[..., None]
    masked = inputs * filled
    wide = jnp.broadcast_to(filled, (*occupancy.shape, 128))
    bordered = with_halo(masked, ((GX, 0), ("gy", 1)), 1)
    grid_up, term = run_first(bordered, cotangent, wide, weight)
    row_sums = sum_by_axis(term, GX, 0)
    border_up = with_halo(grid_up, ((GX, 0), ("gy", 1)), 1)
    input_grad = run_second(border_up, wide, weight)
    weight_grad = sent_and_summed(row_sums, "gy", 1)
    return (input_grad, weight_grad)


def solution(mesh):
    split_mesh = Mesh(mesh.devices.reshape(4, 4, mesh.shape["gy"]), ("gx_0", "gx_1", "gy"))
    in_specs = (P(GX, "gy", None, None), P(GX, "gy", None, None), P(), P(GX, "gy", None))
    out_specs = (P(GX, "gy", None, None), P(GX, "gy"))
    return jax.shard_map(body, mesh=split_mesh, in_specs=in_specs, out_specs=out_specs, check_vma=False)
```

time: 331 us -> 220 us (0.66)
  the two profiles are of different devices: /device:TPU:0 before, /device:TPU:1 now
where the time goes in v1:
time: 220 us; the launch traced here: 219 us
  waiting for transfers between devices  113 us (51%)
  Pallas kernels  56.4 us (26%)
  starting transfers between devices  27.3 us (12%)
  between operations  14.2 us (6%)
  other arithmetic  5.62 us (3%)
  local copies, waits for them, and re-layouts  3.23 us (1%)
    reduce_scatter x2, waiting for transfers between devices, sum_by_axis(): array = lax.psum_scatter(array, axis, scatter_dimension=dim, tiled=True)  94.1 us
    pallas_call x1, Pallas kernels, run_first(): pl.pallas_call(first_kernel, out_shape=(jax.ShapeDtypeStruct((8, 8, 16, 2...  38 us
    pallas_call x1, Pallas kernels, run_second(): pl.pallas_call(second_kernel, out_shape=jax.ShapeDtypeStruct((8, 8, 16, 2...  18.4 us
    ppermute x4, starting transfers between devices, with_halo(): before = lax.ppermute(last, axis, up)  15.8 us
    ppermute x4, waiting for transfers between devices, with_halo(): after = lax.ppermute(first, axis, down)  13.8 us
    ppermute x4, starting transfers between devices, with_halo(): after = lax.ppermute(first, axis, down)  6.43 us
    all_to_all x1, starting transfers between devices, sent_and_summed(): lax.all_to_all(cut_along(array, dim, devices), axis, 0, 0, tiled=True)  5 us
    ppermute x4, waiting for transfers between devices, with_halo(): before = lax.ppermute(last, axis, up)  4.61 us
  transfers between devices with their start and end apart: 11, of which 10 were waited for; matrix products, arithmetic and copies ran while one was open for 1% of the time, Pallas kernels for 8%

profile of v1, /device:TPU:1, one launch (start us, length us, event | category | flops | bytes accessed | tf_op | source)
XLA Modules:
  0.0 219.3 jit_solution(12309152006275018904)
XLA Ops:
  7.2 0.0 reduce-scatter.3.cloned.1.call-start
  7.2 0.8 convert_element_type.3
  8.0 1.4 broadcast_multiply_fusion
  9.4 3.9 %collective-permute-start = (f32[1,8,16,256]{3,2,1,0:T(8,128)S(1)}, f32[1,8,16,256]{3,2,1,0:T(8,128)S(1)}, u32[]{:S(2)}, u32[]{:S(2)}) collective-permute-start(f32[1,8,16,256]{3,2,1,0:T(8,128)S(1)} %get-tuple-element.12), channel_id=1, source_target_pairs={{0,8},{8,16},{16,24},{24,32},{32,40},{40,48},{48,56},{56,64},{64,7... | collective-permute-start | bytes 393224 | tf_op jit(solution)/shard_map/ppermute | solution.py:248
  13.4 1.3 collective-permute-start.1
  14.7 0.9 collective-permute-done
  15.5 3.6 %collective-permute-done.1 = f32[1,8,16,256]{3,2,1,0:T(8,128)S(1)} collective-permute-done((f32[1,8,16,256]{3,2,1,0:T(8,128)S(1)}, f32[1,8,16,256]{3,2,1,0:T(8,128)S(1)}, u32[]{:S(2)}, u32[]{:S(2)}) %collective-permute-start.1) | collective-permute-done | bytes 131104 | tf_op jit(solution)/shard_map/ppermute | solution.py:249
  19.1 5.2 %collective-permute-start.2 = (f32[10,1,16,256]{3,2,1,0:T(8,128)S(1)}, f32[10,1,16,256]{3,2,1,0:T(8,128)S(1)}, u32[]{:S(2)}, u32[]{:S(2)}) collective-permute-start(f32[10,1,16,256]{3,2,1,0:T(8,128)S(1)} %get-tuple-element.8), channel_id=1, source_target_pairs={{0,1},{1,2},{2,3},{3,4},{4,5},{5,6},{6,7},{8,9},{9,10},{10,11},{11... | collective-permute-start | bytes 491528 | tf_op jit(solution)/shard_map/ppermute | solution.py:248
  24.3 1.9 collective-permute-start.3
  26.2 0.3 collective-permute-done.2
  26.6 4.4 %collective-permute-done.3 = f32[10,1,16,256]{3,2,1,0:T(8,128)S(1)} collective-permute-done((f32[10,1,16,256]{3,2,1,0:T(8,128)S(1)}, f32[10,1,16,256]{3,2,1,0:T(8,128)S(1)}, u32[]{:S(2)}, u32[]{:S(2)}) %collective-permute-start.3) | collective-permute-done | bytes 163872 | tf_op jit(solution)/shard_map/ppermute | solution.py:249
  31.0 1.4 pad_maximum_fusion.padded
  32.4 1.0 broadcast_in_dim.2.filled
  33.4 38.0 %first.1 = (f32[8,8,16,256]{3,2,1,0:T(8,128)}, f32[6912,256]{1,0:T(8,128)}) custom-call(f32[10,10,16,256]{3,2,1,0:T(8,128)} %pad_maximum_fusion.padded, f32[8,8,16,256]{3,2,1,0:T(8,128)} %cotangent.1, f32[8,8,16,128]{3,2,1,0:T(8,128)} %broadcast_in_dim.2.filled, f32[6912,256]{1,0:T(8,128)} %weight.3), custom_call_target="tpu_custom_call" | custom-call | tf_op jit(solution)/shard_map/first/pallas_call | solution.py:218
  71.4 0.0 reduce-scatter.3.cloned.1.call-update
  71.4 0.0 copy-start
  71.4 0.0 reduce-scatter.5.cloned.1.call-start
  71.5 73.9 %reduce-scatter.3.cloned.1.call-done = f32[1728,256]{1,0:T(8,128)} async-done(((f32[6912,256]{1,0:T(8,128)}), f32[1728,256]{1,0:T(8,128)}) %reduce-scatter.3.cloned.1.call-update) | async-done | bytes 1769488 | tf_op jit(solution)/shard_map/reduce_scatter | solution.py:256
  145.4 0.0 reduce-scatter.5.cloned.1.call-update
  145.5 0.0 copy-done
  145.5 3.1 %collective-permute-start.4 = (f32[1,8,16,256]{3,2,1,0:T(8,128)S(1)}, f32[1,8,16,256]{3,2,1,0:T(8,128)S(1)}, u32[]{:S(2)}, u32[]{:S(2)}) collective-permute-start(f32[1,8,16,256]{3,2,1,0:T(8,128)S(1)} %get-tuple-element.11), channel_id=1, source_target_pairs={{0,8},{8,16},{16,24},{24,32},{32,40},{40,48},{48,56},{56,64},{64,7... | collective-permute-start | bytes 393224 | tf_op jit(solution)/shard_map/ppermute | solution.py:248
  148.6 1.3 collective-permute-start.5
  149.9 0.8 collective-permute-done.4
  150.7 0.1 constant_dynamic-update-slice_fusion.1
  150.8 3.5 %collective-permute-done.5 = f32[1,8,16,256]{3,2,1,0:T(8,128)S(1)} collective-permute-done((f32[1,8,16,256]{3,2,1,0:T(8,128)S(1)}, f32[1,8,16,256]{3,2,1,0:T(8,128)S(1)}, u32[]{:S(2)}, u32[]{:S(2)}) %collective-permute-start.5) | collective-permute-done | bytes 131104 | tf_op jit(solution)/shard_map/ppermute | solution.py:249
  154.3 20.2 %reduce-scatter.5.cloned.1.call-done = f32[432,256]{1,0:T(8,128)} async-done(((f32[1728,256]{1,0:T(8,128)}), f32[432,256]{1,0:T(8,128)}) %reduce-scatter.5.cloned.1.call-update) | async-done | bytes 442384 | tf_op jit(solution)/shard_map/reduce_scatter | solution.py:256
  174.5 2.0 copy.6
  176.5 5.0 %all-to-all-start = ((f32[8,432,32]{1,2,0:T(8,128)}), f32[8,432,32]{1,2,0:T(8,128)S(1)}, u32[]{:S(2)}, u32[]{:S(2)}) async-start(f32[8,432,32]{1,2,0:T(8,128)} %bitcast.1), calls=%async_computation.2 | async-start | bytes 1048576 | tf_op jit(solution)/shard_map/all_to_all | solution.py:268
  181.6 3.5 %collective-permute-start.6 = (f32[10,1,16,256]{3,2,1,0:T(8,128)S(1)}, f32[10,1,16,256]{3,2,1,0:T(8,128)S(1)}, u32[]{:S(2)}, u32[]{:S(2)}) collective-permute-start(f32[10,1,16,256]{3,2,1,0:T(8,128)S(1)} %get-tuple-element.6), channel_id=1, source_target_pairs={{0,1},{1,2},{2,3},{3,4},{4,5},{5,6},{6,7},{8,9},{9,10},{10,11},{11... | collective-permute-start | bytes 491528 | tf_op jit(solution)/shard_map/ppermute | solution.py:248
  185.1 1.9 collective-permute-start.7
  187.0 2.6 %collective-permute-done.6 = f32[10,1,16,256]{3,2,1,0:T(8,128)S(1)} collective-permute-done((f32[10,1,16,256]{3,2,1,0:T(8,128)S(1)}, f32[10,1,16,256]{3,2,1,0:T(8,128)S(1)}, u32[]{:S(2)}, u32[]{:S(2)}) %collective-permute-start.6) | collective-permute-done | bytes 163872 | tf_op jit(solution)/shard_map/ppermute | solution.py:248
  189.7 2.4 %collective-permute-done.7 = f32[10,1,16,256]{3,2,1,0:T(8,128)S(1)} collective-permute-done((f32[10,1,16,256]{3,2,1,0:T(8,128)S(1)}, f32[10,1,16,256]{3,2,1,0:T(8,128)S(1)}, u32[]{:S(2)}, u32[]{:S(2)}) %collective-permute-start.7) | collective-permute-done | bytes 163872 | tf_op jit(solution)/shard_map/ppermute | solution.py:249
  192.0 1.4 pad_maximum_fusion.1.padded
  193.4 18.4 %second.1 = f32[8,8,16,256]{3,2,1,0:T(8,128)} custom-call(f32[10,10,16,256]{3,2,1,0:T(8,128)} %pad_maximum_fusion.1.padded, f32[8,8,16,128]{3,2,1,0:T(8,128)} %broadcast_in_dim.2.filled, f32[6912,256]{1,0:T(8,128)} %weight.3), custom_call_target="tpu_custom_call" | custom-call | tf_op jit(solution)/shard_map/second/pallas_call | solution.py:230
  211.8 0.0 all-to-all-done
  211.8 0.7 reduce_sum.9
  (6 shorter events, 0.1 us)
Async XLA Ops:
  7.2 138.3 %reduce-scatter.3.cloned.1.call-start = ((), (), s32[]{:S(2)}) async-start(), calls=%async_computation.3 | async-start | bytes 8847360 | tf_op jit(solution)/shard_map/reduce_scatter | solution.py:256
  9.4 6.1 %collective-permute-start = (f32[1,8,16,256]{3,2,1,0:T(8,128)S(1)}, f32[1,8,16,256]{3,2,1,0:T(8,128)S(1)}, u32[]{:S(2)}, u32[]{:S(2)}) collective-permute-start(f32[1,8,16,256]{3,2,1,0:T(8,128)S(1)} %get-tuple-element.12), channel_id=1, source_target_pairs={{0,8},{8,16},{16,24},{24,32},{32,40},{40,48},{48,56},{56,64},{64,7... | collective-permute-start | bytes 393224 | tf_op jit(solution)/shard_map/ppermute | solution.py:248
  13.4 5.7 %collective-permute-start.1 = (f32[1,8,16,256]{3,2,1,0:T(8,128)S(1)}, f32[1,8,16,256]{3,2,1,0:T(8,128)S(1)}, u32[]{:S(2)}, u32[]{:S(2)}) collective-permute-start(f32[1,8,16,256]{3,2,1,0:T(8,128)S(1)} %get-tuple-element.13), channel_id=1, source_target_pairs={{8,0},{16,8},{24,16},{32,24},{40,32},{48,40},{56,48},{64,56},{72,6... | collective-permute-start | bytes 393224 | tf_op jit(solution)/shard_map/ppermute | solution.py:249
  19.1 7.4 %collective-permute-start.2 = (f32[10,1,16,256]{3,2,1,0:T(8,128)S(1)}, f32[10,1,16,256]{3,2,1,0:T(8,128)S(1)}, u32[]{:S(2)}, u32[]{:S(2)}) collective-permute-start(f32[10,1,16,256]{3,2,1,0:T(8,128)S(1)} %get-tuple-element.8), channel_id=1, source_target_pairs={{0,1},{1,2},{2,3},{3,4},{4,5},{5,6},{6,7},{8,9},{9,10},{10,11},{11... | collective-permute-start | bytes 491528 | tf_op jit(solution)/shard_map/ppermute | solution.py:248
  24.3 6.6 %collective-permute-start.3 = (f32[10,1,16,256]{3,2,1,0:T(8,128)S(1)}, f32[10,1,16,256]{3,2,1,0:T(8,128)S(1)}, u32[]{:S(2)}, u32[]{:S(2)}) collective-permute-start(f32[10,1,16,256]{3,2,1,0:T(8,128)S(1)} %get-tuple-element.9), channel_id=1, source_target_pairs={{1,0},{2,1},{3,2},{4,3},{5,4},{6,5},{7,6},{9,8},{10,9},{11,10},{12... | collective-permute-start | bytes 491528 | tf_op jit(solution)/shard_map/ppermute | solution.py:249
  71.4 74.0 %copy-start = (f32[8,8,16,256]{3,2,1,0:T(8,128)S(1)}, f32[8,8,16,256]{3,2,1,0:T(8,128)}, u32[]{:S(2)}) copy-start(f32[8,8,16,256]{3,2,1,0:T(8,128)} %get-tuple-element.4) | copy-start | bytes 3145732
  71.4 103.1 %reduce-scatter.5.cloned.1.call-start = ((), (), s32[]{:S(2)}) async-start(), calls=%async_computation.4 | async-start | bytes 2211840 | tf_op jit(solution)/shard_map/reduce_scatter | solution.py:256
  145.5 5.2 %collective-permute-start.4 = (f32[1,8,16,256]{3,2,1,0:T(8,128)S(1)}, f32[1,8,16,256]{3,2,1,0:T(8,128)S(1)}, u32[]{:S(2)}, u32[]{:S(2)}) collective-permute-start(f32[1,8,16,256]{3,2,1,0:T(8,128)S(1)} %get-tuple-element.11), channel_id=1, source_target_pairs={{0,8},{8,16},{16,24},{24,32},{32,40},{40,48},{48,56},{56,64},{64,7... | collective-permute-start | bytes 393224 | tf_op jit(solution)/shard_map/ppermute | solution.py:248
  148.6 5.7 %collective-permute-start.5 = (f32[1,8,16,256]{3,2,1,0:T(8,128)S(1)}, f32[1,8,16,256]{3,2,1,0:T(8,128)S(1)}, u32[]{:S(2)}, u32[]{:S(2)}) collective-permute-start(f32[1,8,16,256]{3,2,1,0:T(8,128)S(1)} %get-tuple-element.10), channel_id=1, source_target_pairs={{8,0},{16,8},{24,16},{32,24},{40,32},{48,40},{56,48},{64,56},{72,6... | collective-permute-start | bytes 393224 | tf_op jit(solution)/shard_map/ppermute | solution.py:249
  176.5 35.3 %all-to-all-start = ((f32[8,432,32]{1,2,0:T(8,128)}), f32[8,432,32]{1,2,0:T(8,128)S(1)}, u32[]{:S(2)}, u32[]{:S(2)}) async-start(f32[8,432,32]{1,2,0:T(8,128)} %bitcast.1), calls=%async_computation.2 | async-start | bytes 1048576 | tf_op jit(solution)/shard_map/all_to_all | solution.py:268
  181.6 8.1 %collective-permute-start.6 = (f32[10,1,16,256]{3,2,1,0:T(8,128)S(1)}, f32[10,1,16,256]{3,2,1,0:T(8,128)S(1)}, u32[]{:S(2)}, u32[]{:S(2)}) collective-permute-start(f32[10,1,16,256]{3,2,1,0:T(8,128)S(1)} %get-tuple-element.6), channel_id=1, source_target_pairs={{0,1},{1,2},{2,3},{3,4},{4,5},{5,6},{6,7},{8,9},{9,10},{10,11},{11... | collective-permute-start | bytes 491528 | tf_op jit(solution)/shard_map/ppermute | solution.py:248
  185.1 6.9 %collective-permute-start.7 = (f32[10,1,16,256]{3,2,1,0:T(8,128)S(1)}, f32[10,1,16,256]{3,2,1,0:T(8,128)S(1)}, u32[]{:S(2)}, u32[]{:S(2)}) collective-permute-start(f32[10,1,16,256]{3,2,1,0:T(8,128)S(1)} %get-tuple-element.7), channel_id=1, source_target_pairs={{1,0},{2,1},{3,2},{4,3},{5,4},{6,5},{7,6},{9,8},{10,9},{11,10},{12... | collective-permute-start | bytes 491528 | tf_op jit(solution)/shard_map/ppermute | solution.py:249
Sparse Core Ops, SparseCore 0:
  71.5 73.8 reduce-scatter.2
  147.9 26.5 reduce-scatter.4

commit v2 on v1

v2 whole, which is shorter than its diff:
```python
import jax, jax.numpy as jnp
from jax import lax
from jax.experimental import pallas as pl
from jax.experimental.pallas import tpu as pltpu
from jax.sharding import PartitionSpec as P

F32 = jnp.float32
BF16 = jnp.bfloat16


def split(value):
    high = value.astype(BF16)
    return high, (value - high.astype(F32)).astype(BF16)


def rows(index, size):
    return pl.ds(pl.multiple_of(index * size, size), size)


def filter_points(a, b, c):
    outer, inner = (a + c) * 0.5, b * 0.5
    return a, outer + inner, outer - inner, c


def data_points(a, b, c, d):
    return a - c, b + c, c - b, b - d


def sums_of_points(a, b, c, d):
    return a + b + c, b - c - d


def points_of_pair(a, b):
    return a, a + b, a - b, -b


def taps_of_points(a, b, c, d):
    outer = (b + c) * 0.5
    return a + outer, (b - c) * 0.5, outer + d


def both(function, grid):
    half = list(zip(*[function(*column) for column in zip(*grid)]))
    return [function(*row) for row in half]


def transform_weight(weight, high, low):
    def step(index, carry):
        grid = [
            [weight[pl.ds(pl.multiple_of((3 * a + b) * 768 + index * 16, 16), 16)] for b in range(3)]
            for a in range(3)
        ]
        points = both(filter_points, grid)
        for u in range(4):
            for v in range(4):
                top, rest = split(points[u][v])
                high[4 * u + v, rows(index, 16)] = top
                low[4 * u + v, rows(index, 16)] = rest
        return carry

    lax.fori_loop(0, 48, step, 0)


def transform_data(padded, high, low):
    def step(tile, carry):
        x, y = tile // 4, tile % 4
        grid = [[padded[2 * x + i, 2 * y + j] for j in range(4)] for i in range(4)]
        points = both(data_points, grid)
        zero = jnp.zeros((1, 256), F32)
        for u in range(4):
            for v in range(4):
                mid = points[u][v]
                down = jnp.concatenate([zero, mid[:15]], axis=0)
                up = jnp.concatenate([mid[1:], zero], axis=0)
                for place, piece in enumerate((down, mid, up)):
                    top, rest = split(piece)
                    high[4 * u + v, rows(tile, 16), 256 * place : 256 * place + 256] = top
                    low[4 * u + v, rows(tile, 16), 256 * place : 256 * place + 256] = rest
        return carry

    lax.fori_loop(0, 16, step, 0)


def dots(left_high, left_low, right_high, right_low, numbers):
    dims = (numbers, ((), ()))
    return (
        lax.dot_general(left_high, right_high, dims, preferred_element_type=F32)
        + lax.dot_general(left_low, right_high, dims, preferred_element_type=F32)
        + lax.dot_general(left_high, right_low, dims, preferred_element_type=F32)
    )


def forward(data_high, data_low, filter_high, filter_low, product):
    def step(point, carry):
        product[point] = dots(
            data_high[point], data_low[point], filter_high[point], filter_low[point], ((1,), (0,))
        )
        return carry

    lax.fori_loop(0, 16, step, 0)


def backward(data_high, data_low, filter_high, filter_low, product):
    def step(point, carry):
        u, v = point // 4, point % 4
        u = jnp.where(u == 0, 3, jnp.where(u == 3, 0, u))
        v = jnp.where(v == 0, 3, jnp.where(v == 3, 0, v))
        other = 4 * u + v
        total = None
        for place in range(3):
            lanes = slice(256 * place, 256 * place + 256)
            taps = slice(256 * (2 - place), 256 * (2 - place) + 256)
            term = dots(
                data_high[point, :, lanes],
                data_low[point, :, lanes],
                filter_high[other, taps],
                filter_low[other, taps],
                ((1,), (1,)),
            )
            total = term if total is None else total + term
        product[point] = total
        return carry

    lax.fori_loop(0, 16, step, 0)


def place_lanes(value):
    left, right = value[:, :128], value[:, 128:]
    group = lax.broadcasted_iota(jnp.int32, left.shape, 1) // 32
    left_32, right_32 = pltpu.roll(left, 96, 1), pltpu.roll(right, 32, 1)
    left_64, right_64 = pltpu.roll(left, 64, 1), pltpu.roll(right, 64, 1)
    even = jnp.where(group == 0, left, jnp.where(group == 1, left_32, jnp.where(group == 2, right_64, right_32)))
    odd = jnp.where(group == 0, left_32, jnp.where(group == 1, left_64, jnp.where(group == 2, right_32, right)))
    return jnp.concatenate([even, odd], axis=1)


def transform_filter(weight, high, low):
    def step(index, carry):
        def piece(tap):
            start = tap * 96 + index * 2
            return jnp.concatenate(
                [weight[half, pl.ds(start, 2)].reshape(16, 128) for half in range(2)], axis=1
            )

        points = both(filter_points, [[piece(3 * a + b) for b in range(3)] for a in range(3)])
        for u in range(4):
            for v in range(4):
                top, rest = split(points[u][v])
                high[4 * u + v, rows(index, 16)] = top
                low[4 * u + v, rows(index, 16)] = rest
        return carry

    lax.fori_loop(0, 48, step, 0)


def backward_points(data_high, data_low, filter_high, filter_low, product, first, last):
    def step(point, carry):
        u, v = point // 4, point % 4
        u = jnp.where(u == 0, 3, jnp.where(u == 3, 0, u))
        v = jnp.where(v == 0, 3, jnp.where(v == 3, 0, v))
        other = 4 * u + v
        total = None
        for place in range(3):
            lanes = slice(256 * place, 256 * place + 256)
            taps = slice(256 * (2 - place), 256 * (2 - place) + 256)
            term = dots(
                data_high[point, :, lanes],
                data_low[point, :, lanes],
                filter_high[other, taps],
                filter_low[other, taps],
                ((1,), (1,)),
            )
            total = term if total is None else total + term
        product[point] = total
        return carry

    lax.fori_loop(first, last, step, 0)


def twice(fill):
    return jnp.concatenate([fill, fill], axis=1)


def upstream_of(product, cotangent, filled, grid_up, up_high, up_low):
    def step(tile, carry):
        x, y = tile // 4, tile % 4
        grid = [[product[4 * u + v, rows(tile, 16)] for v in range(4)] for u in range(4)]
        sums = both(sums_of_points, grid)
        pair = []
        for i in range(2):
            line = []
            for j in range(2):
                value = sums[i][j]
                sigma = 1.0 / (1.0 + jnp.exp(-value))
                fill = twice(filled[2 * x + i, 2 * y + j])
                result = cotangent[2 * x + i, 2 * y + j] * sigma * (1.0 + value * (1.0 - sigma)) * fill
                grid_up[2 * x + i + 1, 2 * y + j + 1] = result
                line.append(place_lanes(result))
            pair.append(line)
        points = both(points_of_pair, pair)
        for u in range(4):
            for v in range(4):
                top, rest = split(points[u][v])
                up_high[4 * u + v, rows(tile, 16)] = top
                up_low[4 * u + v, rows(tile, 16)] = rest
        return carry

    lax.fori_loop(0, 16, step, 0)


def weight_points(data_high, data_low, up_high, up_low, product, place, first, count):
    lanes = slice(256 * place, 256 * place + 256)

    def step(index, carry):
        point = first + index
        product[index] = dots(
            data_high[point, :, lanes], data_low[point, :, lanes], up_high[point], up_low[point], ((0,), (0,))
        )
        return carry

    lax.fori_loop(0, count, step, 0)


def store_taps(term, a, place, index, taps, add):
    for b in range(3):
        start = ((3 * a + b) * 3 + place) * 32 + 2 * index
        for half in range(2):
            value = taps[b][:, 128 * half : 128 * half + 128].reshape(2, 8, 128)
            if add:
                value = value + term[half, pl.ds(start, 2)]
            term[half, pl.ds(start, 2)] = value


def middle_taps(product, term, place):
    def step(index, carry):
        one = [product[v, rows(index, 16)] for v in range(4)]
        two = [product[4 + v, rows(index, 16)] for v in range(4)]
        outer = taps_of_points(*[(p + q) * 0.5 for p, q in zip(one, two)])
        inner = taps_of_points(*[(p - q) * 0.5 for p, q in zip(one, two)])
        store_taps(term, 0, place, index, outer, False)
        store_taps(term, 1, place, index, inner, False)
        store_taps(term, 2, place, index, outer, False)
        return carry

    lax.fori_loop(0, 16, step, 0)


def outer_taps(product, term, place, a):
    def step(index, carry):
        taps = taps_of_points(*[product[v, rows(index, 16)] for v in range(4)])
        store_taps(term, a, place, index, taps, True)
        return carry

    lax.fori_loop(0, 16, step, 0)


def result_of(product, filled, result):
    def step(tile, carry):
        x, y = tile // 4, tile % 4
        grid = [[product[4 * u + v, rows(tile, 16)] for v in range(4)] for u in range(4)]
        sums = both(sums_of_points, grid)
        for i in range(2):
            for j in range(2):
                result[2 * x + i, 2 * y + j] = sums[i][j] * twice(filled[2 * x + i, 2 * y + j])
        return carry

    lax.fori_loop(0, 16, step, 0)


def fill_of(occupancy, filled):
    same = lax.broadcasted_iota(jnp.int32, (16, 16), 0) == lax.broadcasted_iota(jnp.int32, (16, 16), 1)

    def step(x, carry):
        level = occupancy[x].astype(F32)
        for y in range(8):
            line = jnp.where(same, jnp.broadcast_to(level[y : y + 1], (16, 16)), 0.0)
            filled[x, y] = jnp.broadcast_to(jnp.sum(line, axis=1, keepdims=True), (16, 128))
        return carry

    lax.fori_loop(0, 8, step, 0)


def mask_data(padded, filled):
    def step(index, carry):
        x, y = index // 8, index % 8
        padded[x + 1, y + 1] = padded[x + 1, y + 1] * twice(filled[x, y])
        return carry

    lax.fori_loop(0, 64, step, 0)


MESH = pl.DeviceIdType.MESH
AROUND = [(i, j) for i in (-1, 0, 1) for j in (-1, 0, 1) if (i, j) != (0, 0)]


def strip(step):
    source = {-1: 1, 0: pl.ds(1, 8), 1: 8}[step]
    target = {-1: 9, 0: pl.ds(1, 8), 1: 0}[step]
    return source, target


def border_copies(grid, send, recv, gx, gy):
    copies = []
    for index, (i, j) in enumerate(AROUND):
        (from_x, to_x), (from_y, to_y) = strip(i), strip(j)
        copies.append(
            pltpu.make_async_remote_copy(
                grid.at[from_x, from_y],
                grid.at[to_x, to_y],
                send.at[index],
                recv.at[index],
                device_id=((gx + i + 16) % 16, (gy + j + 8) % 8),
                device_id_type=MESH,
            )
        )
    return copies


def clear_edges(grid, gx, gy):
    @pl.when(gx == 0)
    def _():
        grid[0] = jnp.zeros((10, 16, 256), F32)

    @pl.when(gx == 15)
    def _():
        grid[9] = jnp.zeros((10, 16, 256), F32)

    @pl.when(gy == 0)
    def _():
        for x in range(10):
            grid[x, 0] = jnp.zeros((16, 256), F32)

    @pl.when(gy == 7)
    def _():
        for x in range(10):
            grid[x, 9] = jnp.zeros((16, 256), F32)


def kernel(
    inputs, cotangent, weight, occupancy, result, weight_grad,
    term, fh, fl, dh, dl, eh, el, product, padded, padded_up, cot, filled, occ,
    from_core, ring_slots, cross_first, cross_next, packed, packed_in, out, final,
    local, border_send, border_recv, up_send, up_recv, core_send, core_recv,
    ring_send, ring_recv, cross_send, cross_recv, column_send, column_recv,
):
    gx, gy = lax.axis_index("gx"), lax.axis_index("gy")
    z, x, y, c = gx // 4, gx % 4, gy // 2, gy % 2

    load_inputs = pltpu.make_async_copy(inputs, padded.at[pl.ds(1, 8), pl.ds(1, 8)], local.at[0])
    load_occ = pltpu.make_async_copy(occupancy, occ, local.at[1])
    load_weight = [
        pltpu.make_async_copy(weight.at[:, :, pl.ds(128 * half, 128)], term.at[half], local.at[2 + half])
        for half in range(2)
    ]
    load_cot = pltpu.make_async_copy(cotangent, cot, local.at[4])
    for copy in (load_occ, load_inputs, *load_weight, load_cot):
        copy.start()

    def at(new_z, new_x, new_y):
        return (4 * ((new_z + 4) % 4) + (new_x + 4) % 4, 2 * ((new_y + 4) % 4) + c)

    partners = [((gx + i + 16) % 16, (gy + j + 8) % 8) for i, j in AROUND]
    partners += [(gx, 2 * y + 1 - c)]
    partners += [at(z + 1, x, y), at(z - 1, x, y), at(z, x + 1, y), at(z, x - 1, y)]
    partners += [at(z, x, y + 1), at(z, x, y + 2), at(z, x, y + 3)]
    barrier = pltpu.get_barrier_semaphore()
    for partner in partners:
        pl.semaphore_signal(barrier, inc=1, device_id=partner, device_id_type=MESH)

    load_occ.wait()
    fill_of(occ, filled)
    load_inputs.wait()
    mask_data(padded, filled)
    pl.semaphore_wait(barrier, len(partners))
    borders = border_copies(padded, border_send, border_recv, gx, gy)
    for copy in borders:
        copy.start()
    for copy in load_weight:
        copy.wait()
    transform_filter(term, fh, fl)
    for copy in borders:
        copy.wait()
    clear_edges(padded, gx, gy)
    transform_data(padded, dh, dl)
    forward(dh, dl, fh, fl, product)
    load_cot.wait()
    upstream_of(product, cot, filled, padded_up, eh, el)
    borders = border_copies(padded_up, up_send, up_recv, gx, gy)
    for copy in borders:
        copy.start()

    def to_core(a):
        taps = pl.ds(288 * a, 288)
        return pltpu.make_async_remote_copy(
            term.at[1 - c, taps], from_core.at[taps], core_send.at[a], core_recv.at[a],
            device_id=(gx, 2 * y + 1 - c), device_id_type=MESH,
        )

    def add_core(a):
        def step(index, carry):
            tiles = pl.ds(288 * a + 16 * index, 16)
            term[c, tiles] = term[c, tiles] + from_core[tiles]
            return carry

        lax.fori_loop(0, 18, step, 0)

    core_copies = {}
    for a, first, count in ((1, 4, 8), (0, 0, 4), (2, 12, 4)):
        for place in range(3):
            weight_points(dh, dl, eh, el, product, place, first, count)
            if a == 1:
                middle_taps(product, term, place)
            else:
                outer_taps(product, term, place, a)
        core_copies[a] = to_core(a)
        core_copies[a].start()
    for a in (1, 0, 2):
        core_copies[a].wait_recv()
        add_core(a)

    def tiles_of(path, ring, cross, start=0, size=27):
        block = 4 * ((ring + 4) % 4) + cross % 4 if path == 0 else 4 * (cross % 4) + (ring + 4) % 4
        return pl.ds(27 * (2 * block + path) + start, size)

    mine = (z, x)
    other = (x, z)

    def beside(path, step):
        return at(z + step, x, y) if path == 0 else at(z, x + step, y)

    def ring_copy(path, ring, cross, slot, step):
        return pltpu.make_async_remote_copy(
            term.at[c, tiles_of(path, ring, cross)], ring_slots.at[path, slot],
            ring_send.at[path, slot], ring_recv.at[path, slot],
            device_id=beside(path, step), device_id_type=MESH,
        )

    def add_ring(path, ring, cross, slots):
        tiles = tiles_of(path, ring, cross)
        value = term[c, tiles]
        for slot in slots:
            value = value + ring_slots[path, slot]
        term[c, tiles] = value

    ring = [{}, {}]
    order = [(0, 2), (1, 3)]
    for low, high in order:
        for path in range(2):
            r = mine[path]
            ring[path][low] = ring_copy(path, r + 2, low, low, 1)
            ring[path][high] = ring_copy(path, r + 2, high, high, -1)
            ring[path][low].start()
            ring[path][high].start()
    for low, high in order:
        for path in range(2):
            r = mine[path]
            ring[path][4 + high] = ring_copy(path, r + 1, high, 4 + high, 1)
            ring[path][8 + low] = ring_copy(path, r - 1, low, 8 + low, -1)
            ring[path][4 + high].start()
            ring[path][8 + low].start()

    for copy in borders:
        copy.wait()
    clear_edges(padded_up, gx, gy)
    transform_data(padded_up, dh, dl)

    for low, high in order:
        for path in range(2):
            r = mine[path]
            ring[path][low].wait_recv()
            add_ring(path, r + 1, low, (low,))
            ring[path][4 + low] = ring_copy(path, r + 1, low, 4 + low, 1)
            ring[path][4 + low].start()
            ring[path][high].wait_recv()
            add_ring(path, r - 1, high, (high,))
            ring[path][8 + high] = ring_copy(path, r - 1, high, 8 + high, -1)
            ring[path][8 + high].start()

    backward_points(dh, dl, fh, fl, product, 0, 16)

    for path in range(2):
        for slot in range(4, 12):
            ring[path][slot].wait_recv()
    for path in range(2):
        for cross in range(4):
            add_ring(path, mine[path], cross, (4 + cross, 8 + cross))

    def cross_copy(path, target, start, size, slots, index, step):
        q = other[path]
        return pltpu.make_async_remote_copy(
            term.at[c, tiles_of(path, mine[path], q + target + 4, start, size)], slots.at[pl.ds(start, size)],
            cross_send.at[path, index], cross_recv.at[path, index],
            device_id=beside(1 - path, step), device_id_type=MESH,
        )

    cross = [{}, {}]
    for path in range(2):
        plan = [
            (2, 0, 13, cross_first.at[path], 0, 1),
            (2, 13, 14, cross_first.at[path], 1, -1),
            (1, 13, 14, cross_next.at[path, 0], 2, 1),
            (-1, 0, 13, cross_next.at[path, 1], 3, -1),
        ]
        for target, start, size, slots, index, step in plan:
            cross[path][index] = cross_copy(path, target, start, size, slots, index, step)
            cross[path][index].start()
    result_of(product, filled, out)
    store = pltpu.make_async_copy(out, result, local.at[5])
    store.start()
    for path in range(2):
        for target, start, size, index, later, step in ((1, 0, 13, 0, 4, 1), (-1, 13, 14, 1, 5, -1)):
            cross[path][index].wait_recv()
            tiles = tiles_of(path, mine[path], other[path] + target + 4, start, size)
            term[c, tiles] = term[c, tiles] + cross_first[path, pl.ds(start, size)]
            slots = cross_next.at[path, 0 if step == 1 else 1]
            cross[path][later] = cross_copy(path, target, start, size, slots, later, step)
            cross[path][later].start()
    for path in range(2):
        for index in range(2, 6):
            cross[path][index].wait_recv()
        tiles = tiles_of(path, mine[path], other[path])
        final[pl.ds(27 * path, 27)] = term[c, tiles] + cross_next[path, 0] + cross_next[path, 1]

    final[pl.ds(54, 2)] = jnp.zeros((2, 8, 128), F32)
    group = lax.broadcasted_iota(jnp.int32, (8, 128), 1) // 32

    def pack(index, carry):
        parts = [final[4 * index + q] for q in range(4)]
        for target in range(4):
            moved = [
                part if q == target else pltpu.roll(part, (32 * (q - target)) % 128, 1) for q, part in enumerate(parts)
            ]
            packed[target, index] = jnp.where(
                group == 0, moved[0], jnp.where(group == 1, moved[1], jnp.where(group == 2, moved[2], moved[3]))
            )
        return carry

    lax.fori_loop(0, 14, pack, 0)
    columns = []
    for step in (2, 1, 3):
        copy = pltpu.make_async_remote_copy(
            packed.at[(y + step) % 4], packed_in.at[step - 1], column_send.at[step - 1], column_recv.at[step - 1],
            device_id=at(z, x, y + step), device_id_type=MESH,
        )
        copy.start()
        columns.append(copy)
    for copy in columns:
        copy.wait_recv()

    def unpack(index, carry):
        total = packed[y, index] + packed_in[0, index] + packed_in[1, index] + packed_in[2, index]
        for q in range(4):
            moved = total if q == 0 else pltpu.roll(total, 128 - 32 * q, 1)
            weight_grad[4 * index + q] = moved[:, :32]
        return carry

    lax.fori_loop(0, 13, unpack, 0)
    total = packed[y, 13] + packed_in[0, 13] + packed_in[1, 13] + packed_in[2, 13]
    weight_grad[52] = total[:, :32]
    weight_grad[53] = pltpu.roll(total, 96, 1)[:, :32]

    store.wait()
    for copy in core_copies.values():
        copy.wait_send()
    for path in range(2):
        for copy in ring[path].values():
            copy.wait_send()
        for copy in cross[path].values():
            copy.wait_send()
    for copy in columns:
        copy.wait_send()


def body(inputs, cotangent, weight, occupancy):
    anywhere = pl.BlockSpec(memory_space=pl.ANY)
    dma = pltpu.SemaphoreType.DMA
    result, weight_grad = pl.pallas_call(
        kernel,
        out_shape=(
            jax.ShapeDtypeStruct((8, 8, 16, 256), F32),
            jax.ShapeDtypeStruct((54, 8, 32), F32),
        ),
        in_specs=[anywhere] * 4,
        out_specs=(anywhere, pl.BlockSpec(memory_space=pltpu.VMEM)),
        scratch_shapes=[
            pltpu.VMEM((2, 864, 8, 128), F32),
            pltpu.VMEM((16, 768, 256), BF16),
            pltpu.VMEM((16, 768, 256), BF16),
            pltpu.VMEM((16, 256, 768), BF16),
            pltpu.VMEM((16, 256, 768), BF16),
            pltpu.VMEM((16, 256, 256), BF16),
            pltpu.VMEM((16, 256, 256), BF16),
            pltpu.VMEM((16, 256, 256), F32),
            pltpu.VMEM((10, 10, 16, 256), F32),
            pltpu.VMEM((10, 10, 16, 256), F32),
            pltpu.VMEM((8, 8, 16, 256), F32),
            pltpu.VMEM((8, 8, 16, 128), F32),
            pltpu.VMEM((8, 8, 16), jnp.int32),
            pltpu.VMEM((864, 8, 128), F32),
            pltpu.VMEM((2, 12, 27, 8, 128), F32),
            pltpu.VMEM((2, 27, 8, 128), F32),
            pltpu.VMEM((2, 2, 27, 8, 128), F32),
            pltpu.VMEM((4, 14, 8, 128), F32),
            pltpu.VMEM((3, 14, 8, 128), F32),
            pltpu.VMEM((8, 8, 16, 256), F32),
            pltpu.VMEM((56, 8, 128), F32),
            dma((6,)), dma((8,)), dma((8,)), dma((8,)), dma((8,)), dma((3,)), dma((3,)),
            dma((2, 12)), dma((2, 12)), dma((2, 6)), dma((2, 6)), dma((3,)), dma((3,)),
        ],
        compiler_params=pltpu.CompilerParams(
            vmem_limit_bytes=63 << 20, collective_id=0, has_side_effects=True
        ),
        name="voxels",
    )(inputs, cotangent, weight.reshape(864, 8, 256), occupancy)
    return result, weight_grad.reshape(432, 32)


def solution(mesh):
    in_specs = (P("gx", "gy", None, None), P("gx", "gy", None, None), P(), P("gx", "gy", None))
    out_specs = (P("gx", "gy", None, None), P("gx", "gy"))
    return jax.shard_map(body, mesh=mesh, in_specs=in_specs, out_specs=out_specs, check_vma=False)
```

time: 220 us -> 85.4 us (0.39)
  the two profiles are of different devices: /device:TPU:1 before, /device:TPU:0 now
where the time goes in v2:
time: 85.4 us; the launch traced here: 84.5 us
  Pallas kernels  79.9 us (94%)
  local copies, waits for them, and re-layouts  3.94 us (5%)
    pallas_call x1, Pallas kernels, body(): pl.pallas_call(kernel, out_shape=(jax.ShapeDtypeStruct((8, 8, 16, 256), F...  79.9 us
    unnamed x2, local copies, waits for them, and re-layouts  3.94 us

profile of v2, /device:TPU:0, one launch (start us, length us, event | category | flops | bytes accessed | tf_op | source)
XLA Modules:
  0.0 84.5 jit_solution(8420338801445031210)
XLA Ops:
  0.6 79.9 %voxels.1 = (f32[8,8,16,256]{3,2,1,0:T(8,128)}, f32[54,8,32]{2,1,0:T(8,128)}) custom-call(f32[8,8,16,256]{3,2,1,0:T(8,128)} %inputs.1, f32[8,8,16,256]{3,2,1,0:T(8,128)} %cotangent.1, f32[864,8,256]{2,1,0:T(8,128)} %bitcast.2, s32[8,8,16]{2,1,0:T(8,128)} %occupancy.1), custom_call_target="tpu_custom_call" | custom-call | tf_op jit(solution)/shard_map/voxels/pallas_call | solution.py:577
  80.6 1.7 %copy.6 = f32[432,32]{0,1:T(8,128)} copy(f32[432,32]{1,0:T(8,128)} %bitcast.3) | data formatting | bytes 110592
  82.2 2.3 %copy.8 = f32[8,8,16,256]{3,2,1,0:T(8,128)} copy(f32[8,8,16,256]{3,2,1,0:T(8,128)} %get-tuple-element.10) | data formatting | bytes 2097152

commit v3 on v2

--- a/solution.py
+++ b/solution.py
@@ -212,13 +212,14 @@
     lanes = slice(256 * place, 256 * place + 256)
 
     def step(index, carry):
-        point = first + index
-        product[index] = dots(
-            data_high[point, :, lanes], data_low[point, :, lanes], up_high[point], up_low[point], ((0,), (0,))
-        )
-        return carry
-
-    lax.fori_loop(0, count, step, 0)
+        for each in range(4):
+            point = first + 4 * index + each
+            product[4 * index + each] = dots(
+                data_high[point, :, lanes], data_low[point, :, lanes], up_high[point], up_low[point], ((0,), (0,))
+            )
+        return carry
+
+    lax.fori_loop(0, count // 4, step, 0)
 
 
 def store_taps(term, a, place, index, taps, add):
@@ -290,6 +291,7 @@
 
 
 MESH = pl.DeviceIdType.MESH
+AXES = (("x", "y", "z"), ("z", "x", "y"), ("y", "z", "x"))
 AROUND = [(i, j) for i in (-1, 0, 1) for j in (-1, 0, 1) if (i, j) != (0, 0)]
 
 
@@ -356,13 +358,35 @@
     for copy in (load_occ, load_inputs, *load_weight, load_cot):
         copy.start()
 
-    def at(new_z, new_x, new_y):
-        return (4 * ((new_z + 4) % 4) + (new_x + 4) % 4, 2 * ((new_y + 4) % 4) + c)
+    place = {"z": z, "x": x, "y": y}
+
+    def at(position):
+        return (4 * position["z"] + position["x"], 2 * position["y"] + c)
+
+    def beside(axis, step):
+        return at({**place, axis: (place[axis] + step + 4) % 4})
+
+    def target_of(a, column):
+        first, second, _ = AXES[a]
+        unit = 16 * a + 4 * place[first] + place[second]
+        return (unit // 3, 2 * column + c), unit % 3
+
+    def source_of(slot, index):
+        unit = 3 * gx + slot
+        a, high, low = unit // 16, (unit % 16) // 4, unit % 4
+        position = {
+            axis: sum(
+                jnp.where(a == part, (high, low, index)[AXES[part].index(axis)], 0) for part in range(3)
+            )
+            for axis in ("z", "x", "y")
+        }
+        return at(position)
 
     partners = [((gx + i + 16) % 16, (gy + j + 8) % 8) for i, j in AROUND]
     partners += [(gx, 2 * y + 1 - c)]
-    partners += [at(z + 1, x, y), at(z - 1, x, y), at(z, x + 1, y), at(z, x - 1, y)]
-    partners += [at(z, x, y + 1), at(z, x, y + 2), at(z, x, y + 3)]
+    partners += [beside(axis, step) for axis in ("z", "x", "y") for step in (1, -1)]
+    partners += [target_of(a, column)[0] for a in range(3) for column in range(4)]
+    partners += [source_of(slot, index) for slot in range(3) for index in range(4)]
     barrier = pltpu.get_barrier_semaphore()
     for partner in partners:
         pl.semaphore_signal(barrier, inc=1, device_id=partner, device_id_type=MESH)
@@ -404,171 +428,202 @@
 
         lax.fori_loop(0, 18, step, 0)
 
+    def axes_of(a, path):
+        first, second, _ = AXES[a]
+        return (first, second) if path == 0 else (second, first)
+
+    def tiles_of(a, path, ring, cross, start=0, size=9):
+        ring, cross = (ring + 4) % 4, (cross + 4) % 4
+        piece = 4 * ring + cross if path == 0 else 4 * cross + ring
+        return pl.ds(288 * a + 18 * piece + 9 * path + start, size)
+
+    started = []
+
+    def ring_copy(a, path, ring, cross, slot, step):
+        which = 2 * a + path
+        copy = pltpu.make_async_remote_copy(
+            term.at[c, tiles_of(a, path, ring, cross)], ring_slots.at[which, slot],
+            ring_send.at[which, slot], ring_recv.at[which, slot],
+            device_id=beside(axes_of(a, path)[0], step), device_id_type=MESH,
+        )
+        copy.start()
+        rings[which][slot] = copy
+        started.append(copy)
+
+    def add_ring(a, path, ring, cross, slots):
+        tiles = tiles_of(a, path, ring, cross)
+        value = term[c, tiles]
+        for slot in slots:
+            value = value + ring_slots[2 * a + path, slot]
+        term[c, tiles] = value
+
+    rings = [{} for _ in range(6)]
+    crossing = [{} for _ in range(6)]
+    order = ((0, 2), (1, 3))
+
+    def ring_first(a):
+        for low, high in order:
+            for path in range(2):
+                r = place[axes_of(a, path)[0]]
+                ring_copy(a, path, r + 2, low, low, 1)
+                ring_copy(a, path, r + 2, high, high, -1)
+        for low, high in order:
+            for path in range(2):
+                r = place[axes_of(a, path)[0]]
+                ring_copy(a, path, r + 1, high, 4 + high, 1)
+                ring_copy(a, path, r - 1, low, 8 + low, -1)
+
+    def ring_second(a):
+        for low, high in order:
+            for path in range(2):
+                r = place[axes_of(a, path)[0]]
+                rings[2 * a + path][low].wait_recv()
+                add_ring(a, path, r + 1, low, (low,))
+                ring_copy(a, path, r + 1, low, 4 + low, 1)
+                rings[2 * a + path][high].wait_recv()
+                add_ring(a, path, r - 1, high, (high,))
+                ring_copy(a, path, r - 1, high, 8 + high, -1)
+
+    def cross_copy(a, path, target, start, size, slots, index, step):
+        which, (along, across) = 2 * a + path, axes_of(a, path)
+        copy = pltpu.make_async_remote_copy(
+            term.at[c, tiles_of(a, path, place[along], place[across] + target, start, size)], slots.at[pl.ds(start, size)],
+            cross_send.at[which, index], cross_recv.at[which, index],
+            device_id=beside(across, step), device_id_type=MESH,
+        )
+        copy.start()
+        crossing[which][index] = copy
+        started.append(copy)
+
+    def ring_last(a):
+        for path in range(2):
+            for slot in range(4, 12):
+                rings[2 * a + path][slot].wait_recv()
+            for cross in range(4):
+                add_ring(a, path, place[axes_of(a, path)[0]], cross, (4 + cross, 8 + cross))
+        for path in range(2):
+            which = 2 * a + path
+            cross_copy(a, path, 2, 0, 4, cross_first.at[which], 0, 1)
+            cross_copy(a, path, 2, 4, 5, cross_first.at[which], 1, -1)
+        for path in range(2):
+            which = 2 * a + path
+            cross_copy(a, path, 1, 4, 5, cross_next.at[which, 0], 2, 1)
+            cross_copy(a, path, -1, 0, 4, cross_next.at[which, 1], 3, -1)
+
+    def cross_second(a):
+        for path in range(2):
+            which, (along, across) = 2 * a + path, axes_of(a, path)
+            for target, start, size, index, step in ((1, 0, 4, 0, 1), (-1, 4, 5, 1, -1)):
+                crossing[which][index].wait_recv()
+                tiles = tiles_of(a, path, place[along], place[across] + target, start, size)
+                term[c, tiles] = term[c, tiles] + cross_first[which, pl.ds(start, size)]
+                cross_copy(a, path, target, start, size, cross_next.at[which, index], 4 + index, step)
+
+    group = lax.broadcasted_iota(jnp.int32, (8, 128), 1) // 32
+    columns = []
+
+    def column_copy(a, column):
+        target, slot = target_of(a, column)
+        index = place[AXES[a][2]]
+        here = jnp.logical_and(target[0] == gx, column == y)
+        local_copy = pltpu.make_async_copy(
+            packed.at[a, column], packed_in.at[slot, index], column_recv.at[slot, index]
+        )
+        copy = pltpu.make_async_remote_copy(
+            packed.at[a, column], packed_in.at[slot, index], column_send.at[a, column], column_recv.at[slot, index],
+            device_id=target, device_id_type=MESH,
+        )
+        pl.when(here)(local_copy.start)
+        pl.when(jnp.logical_not(here))(copy.start)
+        columns.append((here, copy))
+
+    def cross_last(a):
+        for path in range(2):
+            which = 2 * a + path
+            for index in range(2, 6):
+                crossing[which][index].wait_recv()
+            along, across = axes_of(a, path)
+            tiles = tiles_of(a, path, place[along], place[across])
+            final[pl.ds(9 * path, 9)] = term[c, tiles] + cross_next[which, 0] + cross_next[which, 1]
+        for index in range(5):
+            parts = [final[min(4 * index + q, 17)] for q in range(4)]
+            for column in range(4):
+                moved = [
+                    part if q == column else pltpu.roll(part, (32 * (q - column)) % 128, 1)
+                    for q, part in enumerate(parts)
+                ]
+                packed[a, column, index] = jnp.where(
+                    group == 0, moved[0], jnp.where(group == 1, moved[1], jnp.where(group == 2, moved[2], moved[3]))
+                )
+        for column in range(4):
+            column_copy(a, column)
+
     core_copies = {}
-    for a, first, count in ((1, 4, 8), (0, 0, 4), (2, 12, 4)):
-        for place in range(3):
-            weight_points(dh, dl, eh, el, product, place, first, count)
+
+    def weight_part(a, first, count):
+        for place_z in range(3):
+            weight_points(dh, dl, eh, el, product, place_z, first, count)
             if a == 1:
-                middle_taps(product, term, place)
+                middle_taps(product, term, place_z)
             else:
-                outer_taps(product, term, place, a)
+                outer_taps(product, term, place_z, a)
         core_copies[a] = to_core(a)
         core_copies[a].start()
-    for a in (1, 0, 2):
+
+    def core_sum(a):
         core_copies[a].wait_recv()
         add_core(a)
 
-    def tiles_of(path, ring, cross, start=0, size=27):
-        block = 4 * ((ring + 4) % 4) + cross % 4 if path == 0 else 4 * (cross % 4) + (ring + 4) % 4
-        return pl.ds(27 * (2 * block + path) + start, size)
-
-    mine = (z, x)
-    other = (x, z)
-
-    def beside(path, step):
-        return at(z + step, x, y) if path == 0 else at(z, x + step, y)
-
-    def ring_copy(path, ring, cross, slot, step):
-        return pltpu.make_async_remote_copy(
-            term.at[c, tiles_of(path, ring, cross)], ring_slots.at[path, slot],
-            ring_send.at[path, slot], ring_recv.at[path, slot],
-            device_id=beside(path, step), device_id_type=MESH,
-        )
-
-    def add_ring(path, ring, cross, slots):
-        tiles = tiles_of(path, ring, cross)
-        value = term[c, tiles]
-        for slot in slots:
-            value = value + ring_slots[path, slot]
-        term[c, tiles] = value
-
-    ring = [{}, {}]
-    order = [(0, 2), (1, 3)]
-    for low, high in order:
-        for path in range(2):
-            r = mine[path]
-            ring[path][low] = ring_copy(path, r + 2, low, low, 1)
-            ring[path][high] = ring_copy(path, r + 2, high, high, -1)
-            ring[path][low].start()
-            ring[path][high].start()
-    for low, high in order:
-        for path in range(2):
-            r = mine[path]
-            ring[path][4 + high] = ring_copy(path, r + 1, high, 4 + high, 1)
-            ring[path][8 + low] = ring_copy(path, r - 1, low, 8 + low, -1)
-            ring[path][4 + high].start()
-            ring[path][8 + low].start()
-
+    weight_part(1, 4, 8)
+    weight_part(0, 0, 4)
+    core_sum(1)
+    ring_first(1)
+    weight_part(2, 12, 4)
+    core_sum(0)
+    ring_first(0)
     for copy in borders:
         copy.wait()
     clear_edges(padded_up, gx, gy)
     transform_data(padded_up, dh, dl)
-
-    for low, high in order:
-        for path in range(2):
-            r = mine[path]
-            ring[path][low].wait_recv()
-            add_ring(path, r + 1, low, (low,))
-            ring[path][4 + low] = ring_copy(path, r + 1, low, 4 + low, 1)
-            ring[path][4 + low].start()
-            ring[path][high].wait_recv()
-            add_ring(path, r - 1, high, (high,))
-            ring[path][8 + high] = ring_copy(path, r - 1, high, 8 + high, -1)
-            ring[path][8 + high].start()
-
-    backward_points(dh, dl, fh, fl, product, 0, 16)
-
-    for path in range(2):
-        for slot in range(4, 12):
-            ring[path][slot].wait_recv()
-    for path in range(2):
-        for cross in range(4):
-            add_ring(path, mine[path], cross, (4 + cross, 8 + cross))
-
-    def cross_copy(path, target, start, size, slots, index, step):
-        q = other[path]
-        return pltpu.make_async_remote_copy(
-            term.at[c, tiles_of(path, mine[path], q + target + 4, start, size)], slots.at[pl.ds(start, size)],
-            cross_send.at[path, index], cross_recv.at[path, index],
-            device_id=beside(1 - path, step), device_id_type=MESH,
-        )
-
-    cross = [{}, {}]
-    for path in range(2):
-        plan = [
-            (2, 0, 13, cross_first.at[path], 0, 1),
-            (2, 13, 14, cross_first.at[path], 1, -1),
-            (1, 13, 14, cross_next.at[path, 0], 2, 1),
-            (-1, 0, 13, cross_next.at[path, 1], 3, -1),
-        ]
-        for target, start, size, slots, index, step in plan:
-            cross[path][index] = cross_copy(path, target, start, size, slots, index, step)
-            cross[path][index].start()
+    core_sum(2)
+    ring_first(2)
+    ring_second(1)
+    ring_second(0)
+    backward_points(dh, dl, fh, fl, product, 0, 4)
+    ring_last(1)
+    ring_second(2)
+    backward_points(dh, dl, fh, fl, product, 4, 8)
+    ring_last(0)
+    cross_second(1)
+    backward_points(dh, dl, fh, fl, product, 8, 12)
+    ring_last(2)
+    cross_second(0)
+    cross_last(1)
+    backward_points(dh, dl, fh, fl, product, 12, 16)
     result_of(product, filled, out)
     store = pltpu.make_async_copy(out, result, local.at[5])
     store.start()
-    for path in range(2):
-        for target, start, size, index, later, step in ((1, 0, 13, 0, 4, 1), (-1, 13, 14, 1, 5, -1)):
-            cross[path][index].wait_recv()
-            tiles = tiles_of(path, mine[path], other[path] + target + 4, start, size)
-            term[c, tiles] = term[c, tiles] + cross_first[path, pl.ds(start, size)]
-            slots = cross_next.at[path, 0 if step == 1 else 1]
-            cross[path][later] = cross_copy(path, target, start, size, slots, later, step)
-            cross[path][later].start()
-    for path in range(2):
-        for index in range(2, 6):
-            cross[path][index].wait_recv()
-        tiles = tiles_of(path, mine[path], other[path])
-        final[pl.ds(27 * path, 27)] = term[c, tiles] + cross_next[path, 0] + cross_next[path, 1]
-
-    final[pl.ds(54, 2)] = jnp.zeros((2, 8, 128), F32)
-    group = lax.broadcasted_iota(jnp.int32, (8, 128), 1) // 32
-
-    def pack(index, carry):
-        parts = [final[4 * index + q] for q in range(4)]
-        for target in range(4):
-            moved = [
-                part if q == target else pltpu.roll(part, (32 * (q - target)) % 128, 1) for q, part in enumerate(parts)
-            ]
-            packed[target, index] = jnp.where(
-                group == 0, moved[0], jnp.where(group == 1, moved[1], jnp.where(group == 2, moved[2], moved[3]))
+    cross_second(2)
+    cross_last(0)
+    cross_last(2)
+    for slot in range(3):
+        for index in range(4):
+            pltpu.make_async_copy(
+                packed.at[0, 0], packed_in.at[slot, index], column_recv.at[slot, index]
+            ).wait()
+    for slot in range(3):
+        for index in range(5):
+            total = (packed_in[slot, 0, index] + packed_in[slot, 1, index]) + (
+                packed_in[slot, 2, index] + packed_in[slot, 3, index]
             )
-        return carry
-
-    lax.fori_loop(0, 14, pack, 0)
-    columns = []
-    for step in (2, 1, 3):
-        copy = pltpu.make_async_remote_copy(
-            packed.at[(y + step) % 4], packed_in.at[step - 1], column_send.at[step - 1], column_recv.at[step - 1],
-            device_id=at(z, x, y + step), device_id_type=MESH,
-        )
-        copy.start()
-        columns.append(copy)
-    for copy in columns:
-        copy.wait_recv()
-
-    def unpack(index, carry):
-        total = packed[y, index] + packed_in[0, index] + packed_in[1, index] + packed_in[2, index]
-        for q in range(4):
-            moved = total if q == 0 else pltpu.roll(total, 128 - 32 * q, 1)
-            weight_grad[4 * index + q] = moved[:, :32]
-        return carry
-
-    lax.fori_loop(0, 13, unpack, 0)
-    total = packed[y, 13] + packed_in[0, 13] + packed_in[1, 13] + packed_in[2, 13]
-    weight_grad[52] = total[:, :32]
-    weight_grad[53] = pltpu.roll(total, 96, 1)[:, :32]
-
+            for q in range(4 if index < 4 else 2):
+                final[18 * slot + 4 * index + q] = total if q == 0 else pltpu.roll(total, 128 - 32 * q, 1)
+    weight_grad[...] = final[...].reshape(448, 128).T[:32, :432]
     store.wait()
-    for copy in core_copies.values():
+    for copy in (*core_copies.values(), *started):
         copy.wait_send()
-    for path in range(2):
-        for copy in ring[path].values():
-            copy.wait_send()
-        for copy in cross[path].values():
-            copy.wait_send()
-    for copy in columns:
-        copy.wait_send()
+    for here, copy in columns:
+        pl.when(jnp.logical_not(here))(copy.wait_send)
 
 
 def body(inputs, cotangent, weight, occupancy):
@@ -578,7 +633,7 @@
         kernel,
         out_shape=(
             jax.ShapeDtypeStruct((8, 8, 16, 256), F32),
-            jax.ShapeDtypeStruct((54, 8, 32), F32),
+            jax.ShapeDtypeStruct((32, 432), F32),
         ),
         in_specs=[anywhere] * 4,
         out_specs=(anywhere, pl.BlockSpec(memory_space=pltpu.VMEM)),
@@ -597,22 +652,22 @@
             pltpu.VMEM((8, 8, 16, 128), F32),
             pltpu.VMEM((8, 8, 16), jnp.int32),
             pltpu.VMEM((864, 8, 128), F32),
-            pltpu.VMEM((2, 12, 27, 8, 128), F32),
-            pltpu.VMEM((2, 27, 8, 128), F32),
-            pltpu.VMEM((2, 2, 27, 8, 128), F32),
-            pltpu.VMEM((4, 14, 8, 128), F32),
-            pltpu.VMEM((3, 14, 8, 128), F32),
+            pltpu.VMEM((6, 12, 9, 8, 128), F32),
+            pltpu.VMEM((6, 9, 8, 128), F32),
+            pltpu.VMEM((6, 2, 9, 8, 128), F32),
+            pltpu.VMEM((3, 4, 5, 8, 128), F32),
+            pltpu.VMEM((3, 4, 5, 8, 128), F32),
             pltpu.VMEM((8, 8, 16, 256), F32),
             pltpu.VMEM((56, 8, 128), F32),
             dma((6,)), dma((8,)), dma((8,)), dma((8,)), dma((8,)), dma((3,)), dma((3,)),
-            dma((2, 12)), dma((2, 12)), dma((2, 6)), dma((2, 6)), dma((3,)), dma((3,)),
+            dma((6, 12)), dma((6, 12)), dma((6, 6)), dma((6, 6)), dma((3, 4)), dma((3, 4)),
         ],
         compiler_params=pltpu.CompilerParams(
             vmem_limit_bytes=63 << 20, collective_id=0, has_side_effects=True
         ),
         name="voxels",
     )(inputs, cotangent, weight.reshape(864, 8, 256), occupancy)
-    return result, weight_grad.reshape(432, 32)
+    return result, weight_grad.T
 
 
 def solution(mesh):

time: 85.4 us -> 73.7 us (0.86)
  Pallas kernels: 79.9 us -> 68.3 us
    pallas_call x1, Pallas kernels: 79.9 us -> 68.3 us  [body(): pl.pallas_call(kernel, out_shape=(jax.ShapeDtypeStruct((8, 8, 16, 256), F...]
where the time goes in v3:
time: 73.7 us; the launch traced here: 72.7 us
  Pallas kernels  68.3 us (93%)
  local copies, waits for them, and re-layouts  3.74 us (5%)
    pallas_call x1, Pallas kernels, body(): pl.pallas_call(kernel, out_shape=(jax.ShapeDtypeStruct((8, 8, 16, 256), F...  68.3 us
    unnamed x2, local copies, waits for them, and re-layouts  3.74 us

profile of v3, /device:TPU:0, one launch (start us, length us, event | category | flops | bytes accessed | tf_op | source)
XLA Modules:
  0.0 72.7 jit_solution(11458296691196486813)
XLA Ops:
  0.6 68.3 %voxels.1 = (f32[8,8,16,256]{3,2,1,0:T(8,128)}, f32[32,432]{1,0:T(8,128)}) custom-call(f32[8,8,16,256]{3,2,1,0:T(8,128)} %inputs.1, f32[8,8,16,256]{3,2,1,0:T(8,128)} %cotangent.1, f32[864,8,256]{2,1,0:T(8,128)} %bitcast.2, s32[8,8,16]{2,1,0:T(8,128)} %occupancy.1), custom_call_target="tpu_custom_call" | custom-call | tf_op jit(solution)/shard_map/voxels/pallas_call | solution.py:632
  69.0 2.3 %copy.8 = f32[8,8,16,256]{3,2,1,0:T(8,128)} copy(f32[8,8,16,256]{3,2,1,0:T(8,128)} %get-tuple-element.8) | data formatting | bytes 2097152
  71.2 1.5 %copy.9 = f32[432,32]{0,1:T(8,128)} copy(f32[432,32]{0,1:T(8,128)} %bitcast.3) | data formatting | bytes 110592

commit v4 on v3

--- a/solution.py
+++ b/solution.py
@@ -44,24 +44,7 @@
     return [function(*row) for row in half]
 
 
-def transform_weight(weight, high, low):
-    def step(index, carry):
-        grid = [
-            [weight[pl.ds(pl.multiple_of((3 * a + b) * 768 + index * 16, 16), 16)] for b in range(3)]
-            for a in range(3)
-        ]
-        points = both(filter_points, grid)
-        for u in range(4):
-            for v in range(4):
-                top, rest = split(points[u][v])
-                high[4 * u + v, rows(index, 16)] = top
-                low[4 * u + v, rows(index, 16)] = rest
-        return carry
-
-    lax.fori_loop(0, 48, step, 0)
-
-
-def transform_data(padded, high, low):
+def data_tiles(padded, high, low, first, last):
     def step(tile, carry):
         x, y = tile // 4, tile % 4
         grid = [[padded[2 * x + i, 2 * y + j] for j in range(4)] for i in range(4)]
@@ -78,7 +61,7 @@
                     low[4 * u + v, rows(tile, 16), 256 * place : 256 * place + 256] = rest
         return carry
 
-    lax.fori_loop(0, 16, step, 0)
+    lax.fori_loop(first, last, step, 0)
 
 
 def dots(left_high, left_low, right_high, right_low, numbers):
@@ -95,30 +78,6 @@
         product[point] = dots(
             data_high[point], data_low[point], filter_high[point], filter_low[point], ((1,), (0,))
         )
-        return carry
-
-    lax.fori_loop(0, 16, step, 0)
-
-
-def backward(data_high, data_low, filter_high, filter_low, product):
-    def step(point, carry):
-        u, v = point // 4, point % 4
-        u = jnp.where(u == 0, 3, jnp.where(u == 3, 0, u))
-        v = jnp.where(v == 0, 3, jnp.where(v == 3, 0, v))
-        other = 4 * u + v
-        total = None
-        for place in range(3):
-            lanes = slice(256 * place, 256 * place + 256)
-            taps = slice(256 * (2 - place), 256 * (2 - place) + 256)
-            term = dots(
-                data_high[point, :, lanes],
-                data_low[point, :, lanes],
-                filter_high[other, taps],
-                filter_low[other, taps],
-                ((1,), (1,)),
-            )
-            total = term if total is None else total + term
-        product[point] = total
         return carry
 
     lax.fori_loop(0, 16, step, 0)
@@ -318,30 +277,44 @@
     return copies
 
 
-def clear_edges(grid, gx, gy):
-    @pl.when(gx == 0)
-    def _():
-        grid[0] = jnp.zeros((10, 16, 256), F32)
-
-    @pl.when(gx == 15)
-    def _():
-        grid[9] = jnp.zeros((10, 16, 256), F32)
-
-    @pl.when(gy == 0)
-    def _():
-        for x in range(10):
-            grid[x, 0] = jnp.zeros((16, 256), F32)
-
-    @pl.when(gy == 7)
-    def _():
-        for x in range(10):
-            grid[x, 9] = jnp.zeros((16, 256), F32)
+def take_sides(grid, copies, gy):
+    for (i, _), copy in zip(AROUND, copies):
+        if i == 0:
+            copy.wait()
+
+    def clear(y):
+        for x in range(1, 9):
+            grid[x, y] = jnp.zeros((16, 256), F32)
+
+    pl.when(gy == 0)(lambda: clear(0))
+    pl.when(gy == 7)(lambda: clear(9))
+
+
+def take_rest(grid, copies, gx, gy):
+    for (i, _), copy in zip(AROUND, copies):
+        if i != 0:
+            copy.wait()
+
+    def clear(x, y):
+        grid[x, y] = jnp.zeros((16, 256), F32)
+
+    def clear_row(x):
+        grid[x] = jnp.zeros((10, 16, 256), F32)
+
+    def clear_corners(y):
+        clear(0, y)
+        clear(9, y)
+
+    pl.when(gx == 0)(lambda: clear_row(0))
+    pl.when(gx == 15)(lambda: clear_row(9))
+    pl.when(gy == 0)(lambda: clear_corners(0))
+    pl.when(gy == 7)(lambda: clear_corners(9))
 
 
 def kernel(
     inputs, cotangent, weight, occupancy, result, weight_grad,
     term, fh, fl, dh, dl, eh, el, product, padded, padded_up, cot, filled, occ,
-    from_core, ring_slots, cross_first, cross_next, packed, packed_in, out, final,
+    from_core, ring_slots, cross_first, cross_next, packed, packed_in, final,
     local, border_send, border_recv, up_send, up_recv, core_send, core_recv,
     ring_send, ring_recv, cross_send, cross_recv, column_send, column_recv,
 ):
@@ -402,10 +375,11 @@
     for copy in load_weight:
         copy.wait()
     transform_filter(term, fh, fl)
-    for copy in borders:
-        copy.wait()
-    clear_edges(padded, gx, gy)
-    transform_data(padded, dh, dl)
+    take_sides(padded, borders, gy)
+    data_tiles(padded, dh, dl, 4, 12)
+    take_rest(padded, borders, gx, gy)
+    data_tiles(padded, dh, dl, 0, 4)
+    data_tiles(padded, dh, dl, 12, 16)
     forward(dh, dl, fh, fl, product)
     load_cot.wait()
     upstream_of(product, cot, filled, padded_up, eh, el)
@@ -413,10 +387,11 @@
     for copy in borders:
         copy.start()
 
-    def to_core(a):
-        taps = pl.ds(288 * a, 288)
+    def to_core(a, place_z, b):
+        index = 9 * a + 3 * place_z + b
+        taps = pl.ds(((3 * a + b) * 3 + place_z) * 32, 32)
         return pltpu.make_async_remote_copy(
-            term.at[1 - c, taps], from_core.at[taps], core_send.at[a], core_recv.at[a],
+            term.at[1 - c, taps], from_core.at[taps], core_send.at[index], core_recv.at[index],
             device_id=(gx, 2 * y + 1 - c), device_id_type=MESH,
         )
 
@@ -560,50 +535,59 @@
 
     core_copies = {}
 
-    def weight_part(a, first, count):
-        for place_z in range(3):
+    def weight_part(a, first, count, places=(0, 1, 2)):
+        for place_z in places:
             weight_points(dh, dl, eh, el, product, place_z, first, count)
             if a == 1:
                 middle_taps(product, term, place_z)
             else:
                 outer_taps(product, term, place_z, a)
-        core_copies[a] = to_core(a)
-        core_copies[a].start()
+            for b in range(3):
+                copy = to_core(a, place_z, b)
+                copy.start()
+                core_copies.setdefault(a, []).append(copy)
 
     def core_sum(a):
-        core_copies[a].wait_recv()
+        for copy in core_copies[a]:
+            copy.wait_recv()
         add_core(a)
 
+    def points(first, last):
+        backward_points(dh, dl, fh, fl, product, first, last)
+
     weight_part(1, 4, 8)
-    weight_part(0, 0, 4)
+    weight_part(0, 0, 4, (0,))
     core_sum(1)
     ring_first(1)
-    weight_part(2, 12, 4)
+    weight_part(0, 0, 4, (1, 2))
+    weight_part(2, 12, 4, (0,))
     core_sum(0)
     ring_first(0)
-    for copy in borders:
-        copy.wait()
-    clear_edges(padded_up, gx, gy)
-    transform_data(padded_up, dh, dl)
+    weight_part(2, 12, 4, (1, 2))
+    ring_second(1)
+    take_sides(padded_up, borders, gy)
+    take_rest(padded_up, borders, gx, gy)
+    data_tiles(padded_up, dh, dl, 0, 5)
     core_sum(2)
     ring_first(2)
-    ring_second(1)
+    data_tiles(padded_up, dh, dl, 5, 16)
     ring_second(0)
-    backward_points(dh, dl, fh, fl, product, 0, 4)
+    points(0, 2)
     ring_last(1)
+    points(2, 4)
     ring_second(2)
-    backward_points(dh, dl, fh, fl, product, 4, 8)
+    points(4, 7)
     ring_last(0)
     cross_second(1)
-    backward_points(dh, dl, fh, fl, product, 8, 12)
+    points(7, 10)
     ring_last(2)
+    cross_last(1)
+    points(10, 12)
     cross_second(0)
-    cross_last(1)
-    backward_points(dh, dl, fh, fl, product, 12, 16)
-    result_of(product, filled, out)
-    store = pltpu.make_async_copy(out, result, local.at[5])
-    store.start()
+    points(12, 14)
     cross_second(2)
+    points(14, 16)
+    result_of(product, filled, result)
     cross_last(0)
     cross_last(2)
     for slot in range(3):
@@ -619,8 +603,7 @@
             for q in range(4 if index < 4 else 2):
                 final[18 * slot + 4 * index + q] = total if q == 0 else pltpu.roll(total, 128 - 32 * q, 1)
     weight_grad[...] = final[...].reshape(448, 128).T[:32, :432]
-    store.wait()
-    for copy in (*core_copies.values(), *started):
+    for copy in (*core_copies[0], *core_copies[1], *core_copies[2], *started):
         copy.wait_send()
     for here, copy in columns:
         pl.when(jnp.logical_not(here))(copy.wait_send)
@@ -632,11 +615,11 @@
     result, weight_grad = pl.pallas_call(
         kernel,
         out_shape=(
-            jax.ShapeDtypeStruct((8, 8, 16, 256), F32),
-            jax.ShapeDtypeStruct((32, 432), F32),
+            pltpu.VMEM((8, 8, 16, 256), F32),
+            pltpu.VMEM((32, 432), F32),
         ),
         in_specs=[anywhere] * 4,
-        out_specs=(anywhere, pl.BlockSpec(memory_space=pltpu.VMEM)),
+        out_specs=(pl.BlockSpec(memory_space=pltpu.VMEM),) * 2,
         scratch_shapes=[
             pltpu.VMEM((2, 864, 8, 128), F32),
             pltpu.VMEM((16, 768, 256), BF16),
@@ -657,13 +640,12 @@
             pltpu.VMEM((6, 2, 9, 8, 128), F32),
             pltpu.VMEM((3, 4, 5, 8, 128), F32),
             pltpu.VMEM((3, 4, 5, 8, 128), F32),
-            pltpu.VMEM((8, 8, 16, 256), F32),
             pltpu.VMEM((56, 8, 128), F32),
-            dma((6,)), dma((8,)), dma((8,)), dma((8,)), dma((8,)), dma((3,)), dma((3,)),
+            dma((5,)), dma((8,)), dma((8,)), dma((8,)), dma((8,)), dma((27,)), dma((27,)),
             dma((6, 12)), dma((6, 12)), dma((6, 6)), dma((6, 6)), dma((3, 4)), dma((3, 4)),
         ],
         compiler_params=pltpu.CompilerParams(
-            vmem_limit_bytes=63 << 20, collective_id=0, has_side_effects=True
+            vmem_limit_bytes=56 << 20, collective_id=0, has_side_effects=True
         ),
         name="voxels",
     )(inputs, cotangent, weight.reshape(864, 8, 256), occupancy)

time: 73.7 us -> 67.3 us (0.913); the launches traced: 72.7 us -> 67.2 us
  Pallas kernels: 68.3 us -> 65 us
  local copies, waits for them, and re-layouts: 3.74 us -> 1.6 us
    pallas_call x1, Pallas kernels: 68.3 us -> 65 us  [body(): pl.pallas_call(kernel, out_shape=(pltpu.VMEM((8, 8, 16, 256), F32), pltpu...]
    unnamed x2, local copies, waits for them, and re-layouts: 3.74 us -> 1.6 us
where the time goes in v4:
time: 67.3 us; the launch traced here: 67.2 us
  Pallas kernels  65 us (97%)
  local copies, waits for them, and re-layouts  1.6 us (2%)
    pallas_call x1, Pallas kernels, body(): pl.pallas_call(kernel, out_shape=(pltpu.VMEM((8, 8, 16, 256), F32), pltpu...  65 us
    unnamed x2, local copies, waits for them, and re-layouts  1.6 us

profile of v4, /device:TPU:0, one launch (start us, length us, event | category | flops | bytes accessed | tf_op | source)
XLA Modules:
  0.0 67.2 jit_solution(4416680528299557302)
XLA Ops:
  0.6 65.0 %voxels.1 = (f32[8,8,16,256]{3,2,1,0:T(8,128)S(1)}, f32[32,432]{1,0:T(8,128)S(1)}) custom-call(f32[8,8,16,256]{3,2,1,0:T(8,128)} %inputs.1, f32[8,8,16,256]{3,2,1,0:T(8,128)} %cotangent.1, f32[864,8,256]{2,1,0:T(8,128)} %bitcast.3, s32[8,8,16]{2,1,0:T(8,128)} %occupancy.1), custom_call_target="tpu_custom_call" | custom-call | tf_op jit(solution)/shard_map/voxels/pallas_call | solution.py:615
  65.6 1.0 %copy.8 = f32[8,8,16,256]{3,2,1,0:T(8,128)} copy(f32[8,8,16,256]{3,2,1,0:T(8,128)S(1)} %get-tuple-element.6) | data formatting | bytes 2097152
  66.6 0.6 copy.9

commit v5 on v4

--- a/solution.py
+++ b/solution.py
@@ -227,14 +227,17 @@
     lax.fori_loop(0, 16, step, 0)
 
 
+def fill_at(level, y):
+    same = lax.broadcasted_iota(jnp.int32, (16, 16), 0) == lax.broadcasted_iota(jnp.int32, (16, 16), 1)
+    line = jnp.where(same, jnp.broadcast_to(level[y : y + 1], (16, 16)), 0.0)
+    return jnp.broadcast_to(jnp.sum(line, axis=1, keepdims=True), (16, 128))
+
+
 def fill_of(occupancy, filled):
-    same = lax.broadcasted_iota(jnp.int32, (16, 16), 0) == lax.broadcasted_iota(jnp.int32, (16, 16), 1)
-
     def step(x, carry):
         level = occupancy[x].astype(F32)
         for y in range(8):
-            line = jnp.where(same, jnp.broadcast_to(level[y : y + 1], (16, 16)), 0.0)
-            filled[x, y] = jnp.broadcast_to(jnp.sum(line, axis=1, keepdims=True), (16, 128))
+            filled[x, y] = fill_at(level, y)
         return carry
 
     lax.fori_loop(0, 8, step, 0)
@@ -254,22 +257,40 @@
 AROUND = [(i, j) for i in (-1, 0, 1) for j in (-1, 0, 1) if (i, j) != (0, 0)]
 
 
-def strip(step):
-    source = {-1: 1, 0: pl.ds(1, 8), 1: 8}[step]
-    target = {-1: 9, 0: pl.ds(1, 8), 1: 0}[step]
-    return source, target
-
-
-def border_copies(grid, send, recv, gx, gy):
+def wait_bytes(ref, semaphore):
+    pltpu.make_async_copy(ref, ref, semaphore).wait()
+
+
+FROM = {-1: lambda start: start, 0: lambda start: pl.ds(start, 8), 1: lambda start: start + 7}
+TO = {-1: 9, 0: pl.ds(1, 8), 1: 0}
+
+
+def border_copies(source, grid, send, side_recv, rest_recv, gx, gy, start=0):
+    copies = []
+    for i, j in AROUND:
+        copies.append(
+            pltpu.make_async_remote_copy(
+                source.at[FROM[i](start), FROM[j](start)],
+                grid.at[TO[i], TO[j]],
+                send,
+                side_recv if i == 0 else rest_recv,
+                device_id=((gx + i + 16) % 16, (gy + j + 8) % 8),
+                device_id_type=MESH,
+            )
+        )
+    return copies
+
+
+def level_copies(occupancy, levels, send, recv, gx, gy):
     copies = []
     for index, (i, j) in enumerate(AROUND):
-        (from_x, to_x), (from_y, to_y) = strip(i), strip(j)
+        rows_x = pl.ds(0, 8) if i == 0 else pl.ds(FROM[i](0), 1)
         copies.append(
             pltpu.make_async_remote_copy(
-                grid.at[from_x, from_y],
-                grid.at[to_x, to_y],
-                send.at[index],
-                recv.at[index],
+                occupancy.at[rows_x],
+                levels.at[index] if i == 0 else levels.at[index, pl.ds(0, 1)],
+                send.at[0 if i == 0 else 1],
+                recv.at[0 if i == 0 else 1],
                 device_id=((gx + i + 16) % 16, (gy + j + 8) % 8),
                 device_id_type=MESH,
             )
@@ -277,10 +298,28 @@
     return copies
 
 
-def take_sides(grid, copies, gy):
-    for (i, _), copy in zip(AROUND, copies):
-        if i == 0:
-            copy.wait()
+def mask_border(grid, levels, index):
+    i, j = AROUND[index]
+
+    def mask(x, y, level, row):
+        grid[x, y] = grid[x, y] * twice(fill_at(level, row))
+
+    if i == 0:
+        for x in range(8):
+            mask(x + 1, TO[j], levels[index, x].astype(F32), FROM[j](0))
+    else:
+        level = levels[index, 0].astype(F32)
+        if j == 0:
+            for y in range(8):
+                mask(TO[i], y + 1, level, y)
+        else:
+            mask(TO[i], TO[j], level, FROM[j](0))
+
+
+def take_sides(grid, gy, masks=None):
+    for index, (i, _) in enumerate(AROUND):
+        if i == 0 and masks:
+            masks(index)
 
     def clear(y):
         for x in range(1, 9):
@@ -290,10 +329,10 @@
     pl.when(gy == 7)(lambda: clear(9))
 
 
-def take_rest(grid, copies, gx, gy):
-    for (i, _), copy in zip(AROUND, copies):
-        if i != 0:
-            copy.wait()
+def take_rest(grid, gx, gy, masks=None):
+    for index, (i, _) in enumerate(AROUND):
+        if i != 0 and masks:
+            masks(index)
 
     def clear(x, y):
         grid[x, y] = jnp.zeros((16, 256), F32)
@@ -314,9 +353,9 @@
 def kernel(
     inputs, cotangent, weight, occupancy, result, weight_grad,
     term, fh, fl, dh, dl, eh, el, product, padded, padded_up, cot, filled, occ,
-    from_core, ring_slots, cross_first, cross_next, packed, packed_in, final,
-    local, border_send, border_recv, up_send, up_recv, core_send, core_recv,
-    ring_send, ring_recv, cross_send, cross_recv, column_send, column_recv,
+    from_core, ring_slots, cross_slots, packed, packed_in, final, across, levels,
+    local, border_sem, core_send, core_recv,
+    ring_send, ring_recv, cross_send, cross_recv, column_send, column_recv, level_send, level_recv,
 ):
     gx, gy = lax.axis_index("gx"), lax.axis_index("gy")
     z, x, y, c = gx // 4, gx % 4, gy // 2, gy % 2
@@ -364,34 +403,42 @@
     for partner in partners:
         pl.semaphore_signal(barrier, inc=1, device_id=partner, device_id_type=MESH)
 
+    pl.semaphore_wait(barrier, len(partners))
+    level_borders = level_copies(occupancy, levels, level_send, level_recv, gx, gy)
+    borders = border_copies(inputs, padded, border_sem.at[0], border_sem.at[1], border_sem.at[2], gx, gy)
+    for copy in (*level_borders, *borders):
+        copy.start()
     load_occ.wait()
     fill_of(occ, filled)
     load_inputs.wait()
     mask_data(padded, filled)
-    pl.semaphore_wait(barrier, len(partners))
-    borders = border_copies(padded, border_send, border_recv, gx, gy)
-    for copy in borders:
-        copy.start()
+
+    def masks(index):
+        mask_border(padded, levels, index)
+
     for copy in load_weight:
         copy.wait()
     transform_filter(term, fh, fl)
-    take_sides(padded, borders, gy)
+    wait_bytes(levels.at[pl.ds(0, 2)], level_recv.at[0])
+    wait_bytes(padded.at[pl.ds(0, 2), pl.ds(0, 8)], border_sem.at[1])
+    take_sides(padded, gy, masks)
     data_tiles(padded, dh, dl, 4, 12)
-    take_rest(padded, borders, gx, gy)
+    wait_bytes(levels.at[0, pl.ds(0, 6)], level_recv.at[1])
+    wait_bytes(padded.at[pl.ds(0, 2), pl.ds(0, 10)], border_sem.at[2])
+    take_rest(padded, gx, gy, masks)
     data_tiles(padded, dh, dl, 0, 4)
     data_tiles(padded, dh, dl, 12, 16)
     forward(dh, dl, fh, fl, product)
     load_cot.wait()
     upstream_of(product, cot, filled, padded_up, eh, el)
-    borders = border_copies(padded_up, up_send, up_recv, gx, gy)
+    borders = border_copies(padded_up, padded_up, border_sem.at[3], border_sem.at[4], border_sem.at[4], gx, gy, 1)
     for copy in borders:
         copy.start()
 
     def to_core(a, place_z, b):
-        index = 9 * a + 3 * place_z + b
         taps = pl.ds(((3 * a + b) * 3 + place_z) * 32, 32)
         return pltpu.make_async_remote_copy(
-            term.at[1 - c, taps], from_core.at[taps], core_send.at[index], core_recv.at[index],
+            term.at[1 - c, taps], from_core.at[taps], core_send, core_recv.at[a],
             device_id=(gx, 2 * y + 1 - c), device_id_type=MESH,
         )
 
@@ -408,22 +455,19 @@
         return (first, second) if path == 0 else (second, first)
 
     def tiles_of(a, path, ring, cross, start=0, size=9):
-        ring, cross = (ring + 4) % 4, (cross + 4) % 4
+        ring, cross = (ring + 4) % 4, cross % 4
         piece = 4 * ring + cross if path == 0 else 4 * cross + ring
         return pl.ds(288 * a + 18 * piece + 9 * path + start, size)
-
-    started = []
 
     def ring_copy(a, path, ring, cross, slot, step):
         which = 2 * a + path
         copy = pltpu.make_async_remote_copy(
             term.at[c, tiles_of(a, path, ring, cross)], ring_slots.at[which, slot],
-            ring_send.at[which, slot], ring_recv.at[which, slot],
+            ring_send, ring_recv.at[which, min(slot, 4)],
             device_id=beside(axes_of(a, path)[0], step), device_id_type=MESH,
         )
         copy.start()
         rings[which][slot] = copy
-        started.append(copy)
 
     def add_ring(a, path, ring, cross, slots):
         tiles = tiles_of(a, path, ring, cross)
@@ -433,7 +477,6 @@
         term[c, tiles] = value
 
     rings = [{} for _ in range(6)]
-    crossing = [{} for _ in range(6)]
     order = ((0, 2), (1, 3))
 
     def ring_first(a):
@@ -459,40 +502,20 @@
                 add_ring(a, path, r - 1, high, (high,))
                 ring_copy(a, path, r - 1, high, 8 + high, -1)
 
-    def cross_copy(a, path, target, start, size, slots, index, step):
-        which, (along, across) = 2 * a + path, axes_of(a, path)
-        copy = pltpu.make_async_remote_copy(
-            term.at[c, tiles_of(a, path, place[along], place[across] + target, start, size)], slots.at[pl.ds(start, size)],
-            cross_send.at[which, index], cross_recv.at[which, index],
-            device_id=beside(across, step), device_id_type=MESH,
-        )
-        copy.start()
-        crossing[which][index] = copy
-        started.append(copy)
-
     def ring_last(a):
         for path in range(2):
-            for slot in range(4, 12):
-                rings[2 * a + path][slot].wait_recv()
+            wait_bytes(ring_slots.at[2 * a + path, pl.ds(4, 8)], ring_recv.at[2 * a + path, 4])
             for cross in range(4):
                 add_ring(a, path, place[axes_of(a, path)[0]], cross, (4 + cross, 8 + cross))
-        for path in range(2):
-            which = 2 * a + path
-            cross_copy(a, path, 2, 0, 4, cross_first.at[which], 0, 1)
-            cross_copy(a, path, 2, 4, 5, cross_first.at[which], 1, -1)
-        for path in range(2):
-            which = 2 * a + path
-            cross_copy(a, path, 1, 4, 5, cross_next.at[which, 0], 2, 1)
-            cross_copy(a, path, -1, 0, 4, cross_next.at[which, 1], 3, -1)
-
-    def cross_second(a):
-        for path in range(2):
-            which, (along, across) = 2 * a + path, axes_of(a, path)
-            for target, start, size, index, step in ((1, 0, 4, 0, 1), (-1, 4, 5, 1, -1)):
-                crossing[which][index].wait_recv()
-                tiles = tiles_of(a, path, place[along], place[across] + target, start, size)
-                term[c, tiles] = term[c, tiles] + cross_first[which, pl.ds(start, size)]
-                cross_copy(a, path, target, start, size, cross_next.at[which, index], 4 + index, step)
+        for step in (2, 1, 3):
+            for path in range(2):
+                which, (along, across) = 2 * a + path, axes_of(a, path)
+                copy = pltpu.make_async_remote_copy(
+                    term.at[c, tiles_of(a, path, place[along], place[across] + step)], cross_slots.at[which, step - 1],
+                    cross_send, cross_recv.at[which],
+                    device_id=beside(across, step), device_id_type=MESH,
+                )
+                copy.start()
 
     group = lax.broadcasted_iota(jnp.int32, (8, 128), 1) // 32
     columns = []
@@ -502,10 +525,10 @@
         index = place[AXES[a][2]]
         here = jnp.logical_and(target[0] == gx, column == y)
         local_copy = pltpu.make_async_copy(
-            packed.at[a, column], packed_in.at[slot, index], column_recv.at[slot, index]
+            packed.at[a, column], packed_in.at[slot, index], column_recv
         )
         copy = pltpu.make_async_remote_copy(
-            packed.at[a, column], packed_in.at[slot, index], column_send.at[a, column], column_recv.at[slot, index],
+            packed.at[a, column], packed_in.at[slot, index], column_send.at[a, column], column_recv,
             device_id=target, device_id_type=MESH,
         )
         pl.when(here)(local_copy.start)
@@ -515,11 +538,12 @@
     def cross_last(a):
         for path in range(2):
             which = 2 * a + path
-            for index in range(2, 6):
-                crossing[which][index].wait_recv()
+            wait_bytes(cross_slots.at[which], cross_recv.at[which])
             along, across = axes_of(a, path)
             tiles = tiles_of(a, path, place[along], place[across])
-            final[pl.ds(9 * path, 9)] = term[c, tiles] + cross_next[which, 0] + cross_next[which, 1]
+            final[pl.ds(9 * path, 9)] = (term[c, tiles] + cross_slots[which, 0]) + (
+                cross_slots[which, 1] + cross_slots[which, 2]
+            )
         for index in range(5):
             parts = [final[min(4 * index + q, 17)] for q in range(4)]
             for column in range(4):
@@ -533,8 +557,6 @@
         for column in range(4):
             column_copy(a, column)
 
-    core_copies = {}
-
     def weight_part(a, first, count, places=(0, 1, 2)):
         for place_z in places:
             weight_points(dh, dl, eh, el, product, place_z, first, count)
@@ -543,13 +565,10 @@
             else:
                 outer_taps(product, term, place_z, a)
             for b in range(3):
-                copy = to_core(a, place_z, b)
-                copy.start()
-                core_copies.setdefault(a, []).append(copy)
+                to_core(a, place_z, b).start()
 
     def core_sum(a):
-        for copy in core_copies[a]:
-            copy.wait_recv()
+        wait_bytes(from_core.at[pl.ds(288 * a, 288)], core_recv.at[a])
         add_core(a)
 
     def points(first, last):
@@ -565,36 +584,32 @@
     ring_first(0)
     weight_part(2, 12, 4, (1, 2))
     ring_second(1)
-    take_sides(padded_up, borders, gy)
-    take_rest(padded_up, borders, gx, gy)
+    wait_bytes(padded_up.at[pl.ds(0, 6), pl.ds(0, 6)], border_sem.at[4])
+    take_sides(padded_up, gy)
+    take_rest(padded_up, gx, gy)
     data_tiles(padded_up, dh, dl, 0, 5)
     core_sum(2)
     ring_first(2)
     data_tiles(padded_up, dh, dl, 5, 16)
     ring_second(0)
-    points(0, 2)
+    points(0, 3)
+    ring_second(2)
+    points(3, 5)
     ring_last(1)
-    points(2, 4)
-    ring_second(2)
-    points(4, 7)
+    points(5, 7)
     ring_last(0)
-    cross_second(1)
-    points(7, 10)
+    points(7, 9)
     ring_last(2)
+    points(9, 11)
     cross_last(1)
-    points(10, 12)
-    cross_second(0)
-    points(12, 14)
-    cross_second(2)
-    points(14, 16)
-    result_of(product, filled, result)
+    points(11, 13)
     cross_last(0)
+    points(13, 16)
     cross_last(2)
-    for slot in range(3):
-        for index in range(4):
-            pltpu.make_async_copy(
-                packed.at[0, 0], packed_in.at[slot, index], column_recv.at[slot, index]
-            ).wait()
+    result_of(product, filled, cot)
+    store = pltpu.make_async_copy(cot, result, local.at[0])
+    store.start()
+    wait_bytes(packed_in, column_recv)
     for slot in range(3):
         for index in range(5):
             total = (packed_in[slot, 0, index] + packed_in[slot, 1, index]) + (
@@ -602,9 +617,18 @@
             )
             for q in range(4 if index < 4 else 2):
                 final[18 * slot + 4 * index + q] = total if q == 0 else pltpu.roll(total, 128 - 32 * q, 1)
-    weight_grad[...] = final[...].reshape(448, 128).T[:32, :432]
-    for copy in (*core_copies[0], *core_copies[1], *core_copies[2], *started):
-        copy.wait_send()
+    across[...] = final[...].reshape(448, 128).T[:32, :432]
+    store_weight = pltpu.make_async_copy(across, weight_grad, local.at[1])
+    store_weight.start()
+    store.wait()
+    store_weight.wait()
+    wait_bytes(levels.at[pl.ds(0, 2)], level_send.at[0])
+    wait_bytes(levels.at[0, pl.ds(0, 6)], level_send.at[1])
+    wait_bytes(padded.at[pl.ds(0, 6), pl.ds(0, 6)], border_sem.at[0])
+    wait_bytes(padded_up.at[pl.ds(0, 6), pl.ds(0, 6)], border_sem.at[3])
+    wait_bytes(from_core, core_send)
+    wait_bytes(ring_slots, ring_send)
+    wait_bytes(cross_slots, cross_send)
     for here, copy in columns:
         pl.when(jnp.logical_not(here))(copy.wait_send)
 
@@ -619,7 +643,7 @@
             pltpu.VMEM((32, 432), F32),
         ),
         in_specs=[anywhere] * 4,
-        out_specs=(pl.BlockSpec(memory_space=pltpu.VMEM),) * 2,
+        out_specs=(anywhere, anywhere),
         scratch_shapes=[
             pltpu.VMEM((2, 864, 8, 128), F32),
             pltpu.VMEM((16, 768, 256), BF16),
@@ -636,13 +660,14 @@
             pltpu.VMEM((8, 8, 16), jnp.int32),
             pltpu.VMEM((864, 8, 128), F32),
             pltpu.VMEM((6, 12, 9, 8, 128), F32),
-            pltpu.VMEM((6, 9, 8, 128), F32),
-            pltpu.VMEM((6, 2, 9, 8, 128), F32),
+            pltpu.VMEM((6, 3, 9, 8, 128), F32),
             pltpu.VMEM((3, 4, 5, 8, 128), F32),
             pltpu.VMEM((3, 4, 5, 8, 128), F32),
             pltpu.VMEM((56, 8, 128), F32),
-            dma((5,)), dma((8,)), dma((8,)), dma((8,)), dma((8,)), dma((27,)), dma((27,)),
-            dma((6, 12)), dma((6, 12)), dma((6, 6)), dma((6, 6)), dma((3, 4)), dma((3, 4)),
+            pltpu.VMEM((32, 432), F32),
+            pltpu.VMEM((8, 8, 8, 16), jnp.int32),
+            dma((5,)), dma((5,)), dma, dma((3,)), dma, dma((6, 5)), dma, dma((6,)),
+            dma((3, 4)), dma, dma((2,)), dma((2,)),
         ],
         compiler_params=pltpu.CompilerParams(
             vmem_limit_bytes=56 << 20, collective_id=0, has_side_effects=True

time: 67.3 us -> 63 us (0.936)
  Pallas kernels: 65 us -> 60.3 us
    pallas_call x1, Pallas kernels: 65 us -> 60.3 us  [body(): pl.pallas_call(kernel, out_shape=(pltpu.VMEM((8, 8, 16, 256), F32), pltpu...]
where the time goes in v5:
time: 63 us; the launch traced here: 62.5 us
  Pallas kernels  60.3 us (96%)
  local copies, waits for them, and re-layouts  1.6 us (3%)
  between operations  0.64 us (1%)
    pallas_call x1, Pallas kernels, body(): pl.pallas_call(kernel, out_shape=(pltpu.VMEM((8, 8, 16, 256), F32), pltpu...  60.3 us
    unnamed x2, local copies, waits for them, and re-layouts  1.6 us

profile of v5, /device:TPU:0, one launch (start us, length us, event | category | flops | bytes accessed | tf_op | source)
XLA Modules:
  0.0 62.5 jit_solution(1369546916146578233)
XLA Ops:
  0.6 60.3 %voxels.1 = (f32[8,8,16,256]{3,2,1,0:T(8,128)S(1)}, f32[32,432]{1,0:T(8,128)S(1)}) custom-call(f32[8,8,16,256]{3,2,1,0:T(8,128)} %inputs.1, f32[8,8,16,256]{3,2,1,0:T(8,128)} %cotangent.1, f32[864,8,256]{2,1,0:T(8,128)} %bitcast.3, s32[8,8,16]{2,1,0:T(8,128)} %occupancy.1), custom_call_target="tpu_custom_call" | custom-call | tf_op jit(solution)/shard_map/voxels/pallas_call | solution.py:639
  60.9 1.0 %copy.8 = f32[8,8,16,256]{3,2,1,0:T(8,128)} copy(f32[8,8,16,256]{3,2,1,0:T(8,128)S(1)} %get-tuple-element.6) | data formatting | bytes 2097152
  61.9 0.6 %copy.9 = f32[432,32]{0,1:T(8,128)} copy(f32[432,32]{0,1:T(8,128)S(1)} %bitcast.2) | data formatting | bytes 110592

commit v6 on v5

--- a/solution.py
+++ b/solution.py
@@ -22,8 +22,9 @@
     return a, outer + inner, outer - inner, c
 
 
-def data_points(a, b, c, d):
-    return a - c, b + c, c - b, b - d
+def data_points(a, b, c, d, only=None):
+    points = (lambda: a - c, lambda: b + c, lambda: c - b, lambda: b - d)
+    return tuple(point() for point in points) if only is None else points[only]()
 
 
 def sums_of_points(a, b, c, d):
@@ -252,6 +253,49 @@
     lax.fori_loop(0, 64, step, 0)
 
 
+def data_task(padded, high, low, u, tile):
+    x, y = tile // 4, tile % 4
+    points = data_points(*[
+        data_points(*[padded[2 * x + i, 2 * y + j] if i in USED[u] else None for i in range(4)], only=u)
+        for j in range(4)
+    ])
+    zero = jnp.zeros((1, 256), F32)
+    for v, mid in enumerate(points):
+        down = jnp.concatenate([zero, mid[:15]], axis=0)
+        up = jnp.concatenate([mid[1:], zero], axis=0)
+        for place, piece in enumerate((down, mid, up)):
+            top, rest = split(piece)
+            high[4 * u + v, 16 * tile : 16 * tile + 16, 256 * place : 256 * place + 256] = top
+            low[4 * u + v, 16 * tile : 16 * tile + 16, 256 * place : 256 * place + 256] = rest
+
+
+USED = ((0, 2), (1, 2), (1, 2), (1, 3))
+
+
+def forward_point(data_high, data_low, filter_high, filter_low, product, point):
+    product[point] = dots(
+        data_high[point], data_low[point], filter_high[point], filter_low[point], ((1,), (0,))
+    )
+
+
+def backward_point(data_high, data_low, filter_high, filter_low, product, point):
+    flip = (3, 1, 2, 0)
+    other = 4 * flip[point // 4] + flip[point % 4]
+    total = None
+    for place in range(3):
+        lanes = slice(256 * place, 256 * place + 256)
+        taps = slice(256 * (2 - place), 256 * (2 - place) + 256)
+        term = dots(
+            data_high[point, :, lanes],
+            data_low[point, :, lanes],
+            filter_high[other, taps],
+            filter_low[other, taps],
+            ((1,), (1,)),
+        )
+        total = term if total is None else total + term
+    product[point] = total
+
+
 MESH = pl.DeviceIdType.MESH
 AXES = (("x", "y", "z"), ("z", "x", "y"), ("y", "z", "x"))
 AROUND = [(i, j) for i in (-1, 0, 1) for j in (-1, 0, 1) if (i, j) != (0, 0)]
@@ -354,7 +398,7 @@
     inputs, cotangent, weight, occupancy, result, weight_grad,
     term, fh, fl, dh, dl, eh, el, product, padded, padded_up, cot, filled, occ,
     from_core, ring_slots, cross_slots, packed, packed_in, final, across, levels,
-    local, border_sem, core_send, core_recv,
+    turns, local, border_sem, core_send, core_recv,
     ring_send, ring_recv, cross_send, cross_recv, column_send, column_recv, level_send, level_recv,
 ):
     gx, gy = lax.axis_index("gx"), lax.axis_index("gy")
@@ -383,31 +427,28 @@
         unit = 16 * a + 4 * place[first] + place[second]
         return (unit // 3, 2 * column + c), unit % 3
 
-    def source_of(slot, index):
-        unit = 3 * gx + slot
-        a, high, low = unit // 16, (unit % 16) // 4, unit % 4
-        position = {
-            axis: sum(
-                jnp.where(a == part, (high, low, index)[AXES[part].index(axis)], 0) for part in range(3)
-            )
-            for axis in ("z", "x", "y")
-        }
-        return at(position)
-
     partners = [((gx + i + 16) % 16, (gy + j + 8) % 8) for i, j in AROUND]
     partners += [(gx, 2 * y + 1 - c)]
     partners += [beside(axis, step) for axis in ("z", "x", "y") for step in (1, -1)]
-    partners += [target_of(a, column)[0] for a in range(3) for column in range(4)]
-    partners += [source_of(slot, index) for slot in range(3) for index in range(4)]
     barrier = pltpu.get_barrier_semaphore()
     for partner in partners:
         pl.semaphore_signal(barrier, inc=1, device_id=partner, device_id_type=MESH)
+
+    near = [beside(axis, step) for axis in ("z", "x", "y") for step in (1, -1)]
+
+    def tell(turn):
+        for partner in near:
+            pl.semaphore_signal(turns.at[turn], inc=1, device_id=partner, device_id_type=MESH)
+
+    def hear(turn):
+        pl.semaphore_wait(turns.at[turn], len(near))
 
     pl.semaphore_wait(barrier, len(partners))
     level_borders = level_copies(occupancy, levels, level_send, level_recv, gx, gy)
     borders = border_copies(inputs, padded, border_sem.at[0], border_sem.at[1], border_sem.at[2], gx, gy)
     for copy in (*level_borders, *borders):
         copy.start()
+    tell(0)
     load_occ.wait()
     fill_of(occ, filled)
     load_inputs.wait()
@@ -422,13 +463,22 @@
     wait_bytes(levels.at[pl.ds(0, 2)], level_recv.at[0])
     wait_bytes(padded.at[pl.ds(0, 2), pl.ds(0, 8)], border_sem.at[1])
     take_sides(padded, gy, masks)
-    data_tiles(padded, dh, dl, 4, 12)
+    inner, outer = list(range(4, 12)), [0, 1, 2, 3, 12, 13, 14, 15]
+    for u in range(2):
+        for tile in inner:
+            data_task(padded, dh, dl, u, tile)
     wait_bytes(levels.at[0, pl.ds(0, 6)], level_recv.at[1])
     wait_bytes(padded.at[pl.ds(0, 2), pl.ds(0, 10)], border_sem.at[2])
     take_rest(padded, gx, gy, masks)
-    data_tiles(padded, dh, dl, 0, 4)
-    data_tiles(padded, dh, dl, 12, 16)
-    forward(dh, dl, fh, fl, product)
+    for tile in outer:
+        data_task(padded, dh, dl, 0, tile)
+    tasks = [[(1, tile) for tile in outer]] + [[(u, tile) for tile in range(16)] for u in (2, 3)] + [[]]
+    for point in range(16):
+        forward_point(dh, dl, fh, fl, product, point)
+        todo = tasks[point // 4]
+        share = len(todo) // 4
+        for u, tile in todo[share * (point % 4) : share * (point % 4 + 1)]:
+            data_task(padded, dh, dl, u, tile)
     load_cot.wait()
     upstream_of(product, cot, filled, padded_up, eh, el)
     borders = border_copies(padded_up, padded_up, border_sem.at[3], border_sem.at[4], border_sem.at[4], gx, gy, 1)
@@ -572,28 +622,42 @@
         add_core(a)
 
     def points(first, last):
-        backward_points(dh, dl, fh, fl, product, first, last)
+        for point in range(first, last):
+            backward_point(dh, dl, fh, fl, product, point)
+            if point < 12:
+                for tile in range(4 * (point % 4), 4 * (point % 4) + 4):
+                    data_task(padded_up, dh, dl, point // 4 + 1, tile)
 
     weight_part(1, 4, 8)
     weight_part(0, 0, 4, (0,))
     core_sum(1)
     ring_first(1)
+    hear(0)
+    tell(1)
     weight_part(0, 0, 4, (1, 2))
     weight_part(2, 12, 4, (0,))
     core_sum(0)
     ring_first(0)
+    hear(1)
+    tell(2)
     weight_part(2, 12, 4, (1, 2))
     ring_second(1)
     wait_bytes(padded_up.at[pl.ds(0, 6), pl.ds(0, 6)], border_sem.at[4])
     take_sides(padded_up, gy)
     take_rest(padded_up, gx, gy)
-    data_tiles(padded_up, dh, dl, 0, 5)
+    for tile in range(8):
+        data_task(padded_up, dh, dl, 0, tile)
     core_sum(2)
     ring_first(2)
-    data_tiles(padded_up, dh, dl, 5, 16)
+    hear(2)
+    tell(3)
+    for tile in range(8, 16):
+        data_task(padded_up, dh, dl, 0, tile)
     ring_second(0)
     points(0, 3)
     ring_second(2)
+    hear(3)
+    tell(4)
     points(3, 5)
     ring_last(1)
     points(5, 7)
@@ -601,6 +665,7 @@
     points(7, 9)
     ring_last(2)
     points(9, 11)
+    hear(4)
     cross_last(1)
     points(11, 13)
     cross_last(0)
@@ -666,7 +731,7 @@
             pltpu.VMEM((56, 8, 128), F32),
             pltpu.VMEM((32, 432), F32),
             pltpu.VMEM((8, 8, 8, 16), jnp.int32),
-            dma((5,)), dma((5,)), dma, dma((3,)), dma, dma((6, 5)), dma, dma((6,)),
+            pltpu.SemaphoreType.REGULAR((5,)), dma((5,)), dma((5,)), dma, dma((3,)), dma, dma((6, 5)), dma, dma((6,)),
             dma((3, 4)), dma, dma((2,)), dma((2,)),
         ],
         compiler_params=pltpu.CompilerParams(

time: 63 us -> 57.5 us (0.913)
  Pallas kernels: 60.3 us -> 54.7 us
    pallas_call x1, Pallas kernels: 60.3 us -> 54.7 us  [body(): pl.pallas_call(kernel, out_shape=(pltpu.VMEM((8, 8, 16, 256), F32), pltpu...]
where the time goes in v6:
time: 57.5 us; the launch traced here: 57 us
  Pallas kernels  54.7 us (95%)
  local copies, waits for them, and re-layouts  1.6 us (3%)
  between operations  0.64 us (1%)
    pallas_call x1, Pallas kernels, body(): pl.pallas_call(kernel, out_shape=(pltpu.VMEM((8, 8, 16, 256), F32), pltpu...  54.7 us
    unnamed x2, local copies, waits for them, and re-layouts  1.6 us

profile of v6, /device:TPU:0, one launch (start us, length us, event | category | flops | bytes accessed | tf_op | source)
XLA Modules:
  0.0 57.0 jit_solution(639664638130245463)
XLA Ops:
  0.6 54.7 %voxels.1 = (f32[8,8,16,256]{3,2,1,0:T(8,128)S(1)}, f32[32,432]{1,0:T(8,128)S(1)}) custom-call(f32[8,8,16,256]{3,2,1,0:T(8,128)} %inputs.1, f32[8,8,16,256]{3,2,1,0:T(8,128)} %cotangent.1, f32[864,8,256]{2,1,0:T(8,128)} %bitcast.3, s32[8,8,16]{2,1,0:T(8,128)} %occupancy.1), custom_call_target="tpu_custom_call" | custom-call | tf_op jit(solution)/shard_map/voxels/pallas_call | solution.py:704
  55.4 1.0 %copy.8 = f32[8,8,16,256]{3,2,1,0:T(8,128)} copy(f32[8,8,16,256]{3,2,1,0:T(8,128)S(1)} %get-tuple-element.6) | data formatting | bytes 2097152
  56.3 0.6 %copy.9 = f32[432,32]{0,1:T(8,128)} copy(f32[432,32]{0,1:T(8,128)S(1)} %bitcast.2) | data formatting | bytes 110592

commit v7 on v6

--- a/solution.py
+++ b/solution.py
@@ -168,18 +168,11 @@
     lax.fori_loop(0, 16, step, 0)
 
 
-def weight_points(data_high, data_low, up_high, up_low, product, place, first, count):
+def weight_point(data_high, data_low, up_high, up_low, product, place, point, slot):
     lanes = slice(256 * place, 256 * place + 256)
-
-    def step(index, carry):
-        for each in range(4):
-            point = first + 4 * index + each
-            product[4 * index + each] = dots(
-                data_high[point, :, lanes], data_low[point, :, lanes], up_high[point], up_low[point], ((0,), (0,))
-            )
-        return carry
-
-    lax.fori_loop(0, count // 4, step, 0)
+    product[slot] = dots(
+        data_high[point, :, lanes], data_low[point, :, lanes], up_high[point], up_low[point], ((0,), (0,))
+    )
 
 
 def store_taps(term, a, place, index, taps, add):
@@ -188,31 +181,23 @@
         for half in range(2):
             value = taps[b][:, 128 * half : 128 * half + 128].reshape(2, 8, 128)
             if add:
-                value = value + term[half, pl.ds(start, 2)]
-            term[half, pl.ds(start, 2)] = value
-
-
-def middle_taps(product, term, place):
-    def step(index, carry):
-        one = [product[v, rows(index, 16)] for v in range(4)]
-        two = [product[4 + v, rows(index, 16)] for v in range(4)]
+                value = value + term[half, start : start + 2]
+            term[half, start : start + 2] = value
+
+
+def taps_task(product, term, a, place, base, index):
+    lines = slice(16 * index, 16 * index + 16)
+    if a == 1:
+        one = [product[base + v, lines] for v in range(4)]
+        two = [product[base + 4 + v, lines] for v in range(4)]
         outer = taps_of_points(*[(p + q) * 0.5 for p, q in zip(one, two)])
         inner = taps_of_points(*[(p - q) * 0.5 for p, q in zip(one, two)])
         store_taps(term, 0, place, index, outer, False)
         store_taps(term, 1, place, index, inner, False)
         store_taps(term, 2, place, index, outer, False)
-        return carry
-
-    lax.fori_loop(0, 16, step, 0)
-
-
-def outer_taps(product, term, place, a):
-    def step(index, carry):
-        taps = taps_of_points(*[product[v, rows(index, 16)] for v in range(4)])
+    else:
+        taps = taps_of_points(*[product[base + v, lines] for v in range(4)])
         store_taps(term, a, place, index, taps, True)
-        return carry
-
-    lax.fori_loop(0, 16, step, 0)
 
 
 def result_of(product, filled, result):
@@ -607,15 +592,22 @@
         for column in range(4):
             column_copy(a, column)
 
-    def weight_part(a, first, count, places=(0, 1, 2)):
-        for place_z in places:
-            weight_points(dh, dl, eh, el, product, place_z, first, count)
-            if a == 1:
-                middle_taps(product, term, place_z)
-            else:
-                outer_taps(product, term, place_z, a)
+    stages = [(a, place_z) for a in (1, 0, 2) for place_z in range(3)]
+
+    def weight_stage(index):
+        points = {1: range(4, 12), 0: range(4), 2: range(12, 16)}[stages[index][0]] if index < 9 else ()
+        share = 16 // max(len(points), 1)
+        for each in range(max(len(points), 1)):
+            if points:
+                slot = 8 * (index % 2) + each
+                weight_point(dh, dl, eh, el, product, stages[index][1], points[each], slot)
+            if index:
+                a, place_z = stages[index - 1]
+                for part in range(share * each, share * each + share):
+                    taps_task(product, term, a, place_z, 8 * ((index - 1) % 2), part)
+        if index:
             for b in range(3):
-                to_core(a, place_z, b).start()
+                to_core(*stages[index - 1], b).start()
 
     def core_sum(a):
         wait_bytes(from_core.at[pl.ds(288 * a, 288)], core_recv.at[a])
@@ -628,52 +620,47 @@
                 for tile in range(4 * (point % 4), 4 * (point % 4) + 4):
                     data_task(padded_up, dh, dl, point // 4 + 1, tile)
 
-    weight_part(1, 4, 8)
-    weight_part(0, 0, 4, (0,))
+    for index in range(7):
+        weight_stage(index)
     core_sum(1)
     ring_first(1)
+    for index in range(7, 10):
+        weight_stage(index)
     hear(0)
     tell(1)
-    weight_part(0, 0, 4, (1, 2))
-    weight_part(2, 12, 4, (0,))
     core_sum(0)
     ring_first(0)
-    hear(1)
-    tell(2)
-    weight_part(2, 12, 4, (1, 2))
-    ring_second(1)
     wait_bytes(padded_up.at[pl.ds(0, 6), pl.ds(0, 6)], border_sem.at[4])
     take_sides(padded_up, gy)
     take_rest(padded_up, gx, gy)
-    for tile in range(8):
+    for tile in range(16):
         data_task(padded_up, dh, dl, 0, tile)
     core_sum(2)
     ring_first(2)
+    points(0, 3)
+    ring_second(1)
+    hear(1)
+    tell(2)
+    points(3, 8)
+    ring_second(0)
     hear(2)
     tell(3)
-    for tile in range(8, 16):
-        data_task(padded_up, dh, dl, 0, tile)
-    ring_second(0)
-    points(0, 3)
+    points(8, 11)
     ring_second(2)
     hear(3)
     tell(4)
-    points(3, 5)
+    points(11, 13)
     ring_last(1)
-    points(5, 7)
+    points(13, 16)
     ring_last(0)
-    points(7, 9)
-    ring_last(2)
-    points(9, 11)
-    hear(4)
-    cross_last(1)
-    points(11, 13)
-    cross_last(0)
-    points(13, 16)
-    cross_last(2)
     result_of(product, filled, cot)
     store = pltpu.make_async_copy(cot, result, local.at[0])
     store.start()
+    ring_last(2)
+    hear(4)
+    cross_last(1)
+    cross_last(0)
+    cross_last(2)
     wait_bytes(packed_in, column_recv)
     for slot in range(3):
         for index in range(5):

time: 57.5 us -> 56.6 us (0.984)
  no operation moved by 1% of the time
where the time goes in v7:
time: 56.6 us; the launch traced here: 56.5 us
  Pallas kernels  54.2 us (96%)
  local copies, waits for them, and re-layouts  1.6 us (3%)
  between operations  0.64 us (1%)
    pallas_call x1, Pallas kernels, body(): pl.pallas_call(kernel, out_shape=(pltpu.VMEM((8, 8, 16, 256), F32), pltpu...  54.2 us
    unnamed x2, local copies, waits for them, and re-layouts  1.6 us

profile of v7, /device:TPU:0, one launch (start us, length us, event | category | flops | bytes accessed | tf_op | source)
XLA Modules:
  0.0 56.5 jit_solution(2443843006665336106)
XLA Ops:
  0.6 54.2 %voxels.1 = (f32[8,8,16,256]{3,2,1,0:T(8,128)S(1)}, f32[32,432]{1,0:T(8,128)S(1)}) custom-call(f32[8,8,16,256]{3,2,1,0:T(8,128)} %inputs.1, f32[8,8,16,256]{3,2,1,0:T(8,128)} %cotangent.1, f32[864,8,256]{2,1,0:T(8,128)} %bitcast.3, s32[8,8,16]{2,1,0:T(8,128)} %occupancy.1), custom_call_target="tpu_custom_call" | custom-call | tf_op jit(solution)/shard_map/voxels/pallas_call | solution.py:691
  54.9 1.0 %copy.8 = f32[8,8,16,256]{3,2,1,0:T(8,128)} copy(f32[8,8,16,256]{3,2,1,0:T(8,128)S(1)} %get-tuple-element.6) | data formatting | bytes 2097152
  55.8 0.6 %copy.9 = f32[432,32]{0,1:T(8,128)} copy(f32[432,32]{0,1:T(8,128)S(1)} %bitcast.2) | data formatting | bytes 110592

commit v8 on v7

--- a/solution.py
+++ b/solution.py
@@ -449,7 +449,7 @@
     wait_bytes(padded.at[pl.ds(0, 2), pl.ds(0, 8)], border_sem.at[1])
     take_sides(padded, gy, masks)
     inner, outer = list(range(4, 12)), [0, 1, 2, 3, 12, 13, 14, 15]
-    for u in range(2):
+    for u in range(3):
         for tile in inner:
             data_task(padded, dh, dl, u, tile)
     wait_bytes(levels.at[0, pl.ds(0, 6)], level_recv.at[1])
@@ -457,7 +457,7 @@
     take_rest(padded, gx, gy, masks)
     for tile in outer:
         data_task(padded, dh, dl, 0, tile)
-    tasks = [[(1, tile) for tile in outer]] + [[(u, tile) for tile in range(16)] for u in (2, 3)] + [[]]
+    tasks = [[(u, tile) for tile in outer] for u in (1, 2)] + [[(3, tile) for tile in range(16)]] + [[]]
     for point in range(16):
         forward_point(dh, dl, fh, fl, product, point)
         todo = tasks[point // 4]

time: 56.6 us -> 56.5 us (level)
  no operation moved by 1% of the time
where the time goes in v8:
time: 56.5 us; the launch traced here: 56.4 us
  Pallas kernels  54.2 us (96%)
  local copies, waits for them, and re-layouts  1.6 us (3%)
  between operations  0.64 us (1%)
    pallas_call x1, Pallas kernels, body(): pl.pallas_call(kernel, out_shape=(pltpu.VMEM((8, 8, 16, 256), F32), pltpu...  54.2 us
    unnamed x2, local copies, waits for them, and re-layouts  1.6 us

profile of v8, /device:TPU:0, one launch (start us, length us, event | category | flops | bytes accessed | tf_op | source)
XLA Modules:
  0.0 56.4 jit_solution(2716459780513944116)
XLA Ops:
  0.6 54.2 %voxels.1 = (f32[8,8,16,256]{3,2,1,0:T(8,128)S(1)}, f32[32,432]{1,0:T(8,128)S(1)}) custom-call(f32[8,8,16,256]{3,2,1,0:T(8,128)} %inputs.1, f32[8,8,16,256]{3,2,1,0:T(8,128)} %cotangent.1, f32[864,8,256]{2,1,0:T(8,128)} %bitcast.3, s32[8,8,16]{2,1,0:T(8,128)} %occupancy.1), custom_call_target="tpu_custom_call" | custom-call | tf_op jit(solution)/shard_map/voxels/pallas_call | solution.py:691
  54.8 1.0 %copy.8 = f32[8,8,16,256]{3,2,1,0:T(8,128)} copy(f32[8,8,16,256]{3,2,1,0:T(8,128)S(1)} %get-tuple-element.6) | data formatting | bytes 2097152
  55.8 0.6 %copy.9 = f32[432,32]{0,1:T(8,128)} copy(f32[432,32]{0,1:T(8,128)S(1)} %bitcast.2) | data formatting | bytes 110592
